TPU v7x, 128 devices: a whole 4x4x4 slice. The times are simulated.
128 devices in a mesh: pos: 16 (over y, z), tile: 8 (over x, core).
Axes of the slice: x: 4, y: 4, z: 4, core: 2. Of those that a mesh axis runs over, the one named last changes fastest.
Arguments:
- object_slices: float32 [2, 2, 4096, 2048], P(None, None, 'pos', 'tile'), may hold values from -4.2 to 4.2
- probe: float32 [2, 256, 256], replicated, may hold values from -6 to 6
- amplitudes: float32 [16, 8, 8, 256, 256], P('pos', 'tile'), may hold values from 0 to 2
- offsets: int32 [16, 8, 8, 2], P('pos', 'tile'), may hold values from -128 to 127, as said below
- counts: int32 [16, 8], P('pos', 'tile'), may hold values from 1 to 8, as said below
Outputs:
- object_grad: float32 [2, 2, 4096, 2048], P(None, None, 'pos', 'tile')
- probe_grad: float32 [2, 256, 256], replicated
Inputs may be any that keep to these rules, and one draw needn't show every extreme that they name: Every patch lies inside the object: offsets are -128 to 127, and 0 or more on the first row or column of tiles, 0 or less on the last. `counts`: some tile has 8 live slots and some tile has one.
All inputs are finite; a program needn't handle non-finite values.
Results may differ from a plain program's by a relative error of at most 0.0003.
Values sent between devices are 32-bit elements; how exact they have to be, the bound alone decides.
No kernel may reach another device: no remote copies, remote signals or barrier semaphores. Data moves between devices by JAX's collectives and lax.ppermute only.
A program may use at most 64 MiB of HBM per device.

v0:
```python
import functools
import itertools
import math

import jax
import jax.numpy as jnp
import numpy as np
from jax import lax
from jax.experimental import pallas as pl
from jax.experimental.pallas import tpu as pltpu
from jax.sharding import Mesh
from jax.sharding import PartitionSpec as P

POS = ("pos_0", "pos_1")
TILE = ("tile_0", "tile_1")
ALL = ("pos_0", "pos_1", "tile_0", "tile_1")
F32 = jnp.float32
BF16 = jnp.bfloat16
ROWS = 32


def real_form(field):
    return np.block([[field.real, field.imag], [-field.imag, field.real]])


def transform_matrices(width):
    half = width // 2
    index = np.arange(width)
    signed = np.where(index < half, index, index - width)
    kernel = np.exp(-1j * 80.0 / (width * width) * signed.astype(np.float64) ** 2)
    impulse = np.fft.ifft(kernel)
    near = np.arange(half)
    gap = (near[:, None] - near[None, :]) % width
    prop_sum = 0.5 * (impulse[gap] + impulse[(gap + half) % width])
    prop_diff = 0.5 * (impulse[gap] - impulse[(gap + half) % width])
    scale = 1.0 / math.sqrt(width)
    even = np.exp(-2j * np.pi / width * (near[:, None] * (2 * near[None, :]) % width)) * scale
    odd = np.exp(-2j * np.pi / width * (near[:, None] * (2 * near[None, :] + 1) % width)) * scale
    return np.stack([real_form(m) for m in (prop_sum, prop_diff, even, odd)])


def halves(matrix):
    high = matrix.astype(np.float32).astype(BF16)
    low = (matrix - high.astype(np.float64)).astype(np.float32).astype(BF16)
    return np.stack([high, low])


def split(value):
    high = value.astype(BF16)
    low = (value - high.astype(F32)).astype(BF16)
    return high, low


def dot(left, right):
    return jnp.dot(left, right, preferred_element_type=F32)


def order_kernel(left_ref, right_ref, perm_ref, out_ref):
    half = left_ref.shape[1] // 2
    for parity in range(2):
        picked = pl.ds(parity, half, stride=2)
        rows = jnp.concatenate([left_ref[0, picked, :], right_ref[0, picked, :]], axis=1)
        first = rows.astype(BF16)
        rest = rows - first.astype(F32)
        second = rest.astype(BF16)
        third = (rest - second.astype(F32)).astype(BF16)
        perm = perm_ref[...]
        out_ref[0, parity] = dot(first, perm) + dot(second, perm) + dot(third, perm)


def ordered(amps):
    slots, width, _ = amps.shape
    index = np.arange(width)
    source = np.where(index < width // 2, 2 * index, 2 * (index - width // 2) + 1)
    perm = (index[:, None] == source[None, :]).astype(BF16)
    return pl.pallas_call(
        order_kernel,
        grid=(slots,),
        in_specs=[
            pl.BlockSpec((1, width, width // 2), lambda i: (i, 0, 0)),
            pl.BlockSpec((1, width, width // 2), lambda i: (i, 0, 1)),
            pl.BlockSpec((width, width), lambda i: (0, 0)),
        ],
        out_specs=pl.BlockSpec((1, 2, width // 2, width), lambda i: (i, 0, 0, 0)),
        out_shape=jax.ShapeDtypeStruct((slots, 2, width // 2, width), F32),
        cost_estimate=pl.CostEstimate(flops=2 * 3 * slots * width**3, bytes_accessed=8 * slots * width**2, transcendentals=0),
        name="order_amps",
    )(amps, amps, jnp.asarray(perm))


def main_kernel(
    count_ref, shift_ref, core_at, odd_at, own_ref, row_a_ref, row_b_ref, in_ref, out_ref, in_ends_ref, out_ends_ref, probe_ref, amps_ref, mats_ref, matts_ref,
    end_in_ref, end_out_ref, side_in_ref, side_out_ref, slab_ref, core_ref, probe_grad_ref,
    ext, gext, rolleds, waves, xas, was, vvs, zzs, amp_ref, mat_ref, matt_ref, sems, amp_sems, out_sems,
):
    half = 128
    grads = [gext.at[j] for j in range(4)]
    copies = []
    for s in range(2):
        for c in range(2):
            for j in range(2):
                copies.append((own_ref.at[s, c, :, pl.ds(j * half, half)], ext.at[1 + j, s, c, pl.ds(half, 2 * half), :]))
    middle = pl.ds(half, 2 * half)
    core, odd = core_at[0], odd_at[0]
    toward_in, toward_out = 3 * (1 - core), 3 * core
    rows_a = pl.ds(pl.multiple_of(3 * half * (1 - odd), half), half)
    rows_b = pl.ds(pl.multiple_of(3 * half * odd, half), half)
    copies.append((row_a_ref, ext.at[1:3, :, :, rows_a, :]))
    copies.append((row_b_ref, ext.at[1:3, :, :, rows_b, :]))
    for j, side, ends in ((toward_in, in_ref, in_ends_ref), (toward_out, out_ref, out_ends_ref)):
        copies.append((side, ext.at[j, :, :, middle, :]))
        copies.append((ends.at[0], ext.at[j, :, :, rows_a, :]))
        copies.append((ends.at[1], ext.at[j, :, :, rows_b, :]))
    copies = [pltpu.make_async_copy(a, b, sems.at[n]) for n, (a, b) in enumerate(copies)]
    copies.append(pltpu.make_async_copy(mats_ref, mat_ref, sems.at[len(copies)]))
    copies.append(pltpu.make_async_copy(matts_ref, matt_ref, sems.at[len(copies)]))
    for copy in copies:
        copy.start()

    def amp_copy(slot):
        return pltpu.make_async_copy(amps_ref.at[slot], amp_ref.at[slot], amp_sems.at[slot])

    for slot in range(8):
        amp_copy(slot).start()
    gext[...] = jnp.zeros_like(gext)
    probe_grad_ref[...] = jnp.zeros_like(probe_grad_ref)
    for copy in copies:
        copy.wait()

    lane = lax.broadcasted_iota(jnp.int32, (ROWS, half), 1)
    tiles = (pl.ds(0, half), pl.ds(half, half))
    count = count_ref[0, 0]

    def phases(which, slot, two):
        rolled, wave, xa, wa, vv, zz = (ref.at[which] for ref in (rolleds, waves, xas, was, vvs, zzs))
        top = shift_ref[slot, 0] + half
        left = shift_ref[slot, 1] + half
        back = lax.rem(2 * half - left, 2 * half)
        masks = (lane >= left, lane + half >= left)

        def patch(s, c, j, r):
            rows = pl.ds(top + r, ROWS)
            return jnp.where(masks[j], ext[j, s, c, rows, :], ext[j + 2, s, c, rows, :])

        def add_grad(s, c, j, r, value):
            rows = pl.ds(top + r, ROWS)
            near, far = grads[j], grads[j + 2]
            near[s, c, rows, :] = near[s, c, rows, :] + jnp.where(masks[j], value, 0.0)
            far[s, c, rows, :] = far[s, c, rows, :] + jnp.where(masks[j], 0.0, value)

        def put(ref, k, r, cols, value):
            high, low = split(value)
            ref[0, k, pl.ds(r, ROWS), cols] = high
            ref[1, k, pl.ds(r, ROWS), cols] = low

        def put_right(r, first, second):
            for c in range(2):
                put(xa, 0, r, tiles[c], first[c] + second[c])
                put(xa, 1, r, tiles[c], first[c] - second[c])

        def right(mats, base):
            def piece(k):
                high, low = mats[0, base + k], mats[1, base + k]
                vv[k] = dot(xa[0, k], high) + dot(xa[1, k], high) + dot(xa[0, k], low)

            return [functools.partial(piece, k) for k in range(2)]

        def left_side(mats, base):
            def piece(k):
                high, low = mats[0, base + k], mats[1, base + k]
                zz[k] = dot(high, wa[0, k]) + dot(high, wa[1, k]) + dot(low, wa[0, k])

            return [functools.partial(piece, k) for k in range(2)]

        def over(piece, *ranges):
            return [functools.partial(piece, *at) for at in itertools.product(*ranges)]

        upper = range(0, half, ROWS)
        all_rows = range(0, 2 * half, ROWS)

        def from_left(h, r, j):
            out = []
            for c in range(2):
                a = zz[0, pl.ds(c * half + r, ROWS), tiles[j]]
                b = zz[1, pl.ds(c * half + r, ROWS), tiles[j]]
                out.append(a - b if h else a + b)
            return out

        def start(r):
            for c in range(2):
                rolled[c, pl.ds(r, ROWS), :] = pltpu.roll(probe_ref[c, pl.ds(r, ROWS), :], left, 1)
            pair = []
            for j in range(2):
                pr, pi = (rolled[c, pl.ds(r, ROWS), tiles[j]] for c in range(2))
                re, im = (patch(0, c, j, r) for c in range(2))
                pair.append((pr * re - pi * im, pr * im + pi * re))
            put_right(r, *pair)

        def turn(r, c):
            ts, td = vv[0, pl.ds(r, ROWS), tiles[c]], vv[1, pl.ds(r, ROWS), tiles[c]]
            bs, bd = vv[0, pl.ds(half + r, ROWS), tiles[c]], vv[1, pl.ds(half + r, ROWS), tiles[c]]
            sum_s, sum_d, dif_s, dif_d = ts + bs, td + bd, ts - bs, td - bd
            put(wa, 0, c * half + r, tiles[0], sum_s + sum_d)
            put(wa, 0, c * half + r, tiles[1], sum_s - sum_d)
            put(wa, 1, c * half + r, tiles[0], dif_s + dif_d)
            put(wa, 1, c * half + r, tiles[1], dif_s - dif_d)

        def exit_wave(h, r):
            row = h * half + r
            pair = []
            for j in range(2):
                wr, wi = from_left(h, r, j)
                wave[0, pl.ds(row, ROWS), tiles[j]] = wr
                wave[1, pl.ds(row, ROWS), tiles[j]] = wi
                re, im = (patch(1, c, j, row) for c in range(2))
                pair.append((wr * re - wi * im, wr * im + wi * re))
            put_right(row, *pair)

        def turn_far(r, c):
            for k in range(2):
                t = vv[k, pl.ds(r, ROWS), tiles[c]]
                b = vv[k, pl.ds(half + r, ROWS), tiles[c]]
                put(wa, 0, c * half + r, tiles[k], t + b)
                put(wa, 1, c * half + r, tiles[k], t - b)

        def compare(k, r):
            for j in range(2):
                fr = zz[k, pl.ds(r, ROWS), tiles[j]]
                fi = zz[k, pl.ds(half + r, ROWS), tiles[j]]
                a = amp_ref[slot, k, pl.ds(r, ROWS), tiles[j]]
                factor = two - two * a * lax.rsqrt(fr * fr + fi * fi + 0.01)
                put(wa, k, r, tiles[j], factor * fr)
                put(wa, k, half + r, tiles[j], factor * fi)

        def turn_back(h, r):
            for k in range(2):
                gr, gi = from_left(h, r, k)
                put(xa, k, h * half + r, tiles[0], gr)
                put(xa, k, h * half + r, tiles[1], gi)

        def grad_late(r):
            pair = []
            for j in range(2):
                grad = []
                for c in range(2):
                    a, b = vv[0, pl.ds(r, ROWS), tiles[c]], vv[1, pl.ds(r, ROWS), tiles[c]]
                    grad.append(a - b if j else a + b)
                gr, gi = grad
                wr, wi = (wave[c, pl.ds(r, ROWS), tiles[j]] for c in range(2))
                add_grad(1, 0, j, r, wr * gr + wi * gi)
                add_grad(1, 1, j, r, wr * gi - wi * gr)
                re, im = (patch(1, c, j, r) for c in range(2))
                pair.append((re * gr + im * gi, re * gi - im * gr))
            put_right(r, *pair)

        def grad_early(h, r):
            row = h * half + r
            terms = ([], [])
            for j in range(2):
                gr, gi = from_left(h, r, j)
                pr, pi = (rolled[c, pl.ds(row, ROWS), tiles[j]] for c in range(2))
                add_grad(0, 0, j, row, pr * gr + pi * gi)
                add_grad(0, 1, j, row, pr * gi - pi * gr)
                re, im = (patch(0, c, j, row) for c in range(2))
                terms[0].append(re * gr + im * gi)
                terms[1].append(re * gi - im * gr)
            for c in range(2):
                term = pltpu.roll(jnp.concatenate(terms[c], axis=1), back, 1)
                probe_grad_ref[c, pl.ds(row, ROWS), :] = probe_grad_ref[c, pl.ds(row, ROWS), :] + term

        pair = range(2)
        return [
            over(start, all_rows),
            right(mat_ref, 0),
            over(turn, upper, pair),
            left_side(matt_ref, 0),
            over(exit_wave, pair, upper),
            right(mat_ref, 2),
            over(turn_far, upper, pair),
            left_side(matt_ref, 2),
            over(compare, pair, upper),
            left_side(mat_ref, 2),
            over(turn_back, pair, upper),
            right(matt_ref, 2),
            over(grad_late, all_rows),
            right(matt_ref, 0),
            over(turn, upper, pair),
            left_side(mat_ref, 0),
            over(grad_early, pair, upper),
        ]

    def visit(step, carry):
        first = 2 * step
        amp_copy(first).wait()
        amp_copy(first + 1).wait()
        live = jnp.where(first + 1 < count, 2.0, 0.0)
        one = phases(0, first, 2.0)
        other = phases(1, jnp.minimum(first + 1, count - 1), live)
        for run in one[0]:
            run()
        for ahead, behind in zip(one[1:], other[:-1]):
            interleave(ahead, behind)
        for run in other[-1]:
            run()
        return carry

    steps = lax.div(count + 1, 2)
    lax.fori_loop(0, steps, visit, 0)

    outer = (pl.ds(0, half), pl.ds(3 * half, half))
    moves = [(gext.at[1:3, :, :, middle, :], core_ref)]
    for j, end, side in ((toward_in, end_in_ref, side_in_ref), (toward_out, end_out_ref, side_out_ref)):
        moves.append((gext.at[j, :, :, middle, :], side))
        for n in range(2):
            moves.append((gext.at[j, :, :, outer[n], :], end.at[n]))
    for n in range(2):
        moves.append((gext.at[1:3, :, :, outer[n], :], slab_ref.at[n]))
    moves = [pltpu.make_async_copy(a, b, out_sems.at[n]) for n, (a, b) in enumerate(moves)]
    for move in moves:
        move.start()

    def leave(slot, carry):
        amp_copy(slot).wait()
        return carry

    lax.fori_loop(2 * steps, 8, leave, 0)
    for move in moves:
        move.wait()


def interleave(first, second):
    at = [((n + 0.5) / len(first), 0, n) for n in range(len(first))]
    at += [((n + 0.5) / len(second), 1, n) for n in range(len(second))]
    for _, which, n in sorted(at):
        (first, second)[which][n]()


def gradients(count, shifts, core, odd, own, row_a, row_b, side_in, side_out, ends_in, ends_out, probe, amps, mats, mats_t):
    width = probe.shape[-1]
    half = width // 2
    shapes = [(2, 2, 2, half, half)] * 2 + [(2, 2, width, half)] * 2 + [(2, 2, 2, 2, half, half), (2, 2, 2, width, half)]
    shapes.append((2, width, width))
    any_space = pl.BlockSpec(memory_space=pl.ANY)
    vmem = pl.BlockSpec(memory_space=pltpu.VMEM)
    smem = pl.BlockSpec(memory_space=pltpu.SMEM)
    return pl.pallas_call(
        main_kernel,
        in_specs=[smem] * 4 + [any_space] * 7 + [vmem] + [any_space] * 3,
        out_specs=[any_space] * 6 + [vmem],
        out_shape=[jax.ShapeDtypeStruct(shape, F32) for shape in shapes],
        scratch_shapes=[
            pltpu.VMEM((4, 2, 2, 4 * half, half), F32),
            pltpu.VMEM((4, 2, 2, 4 * half, half), F32),
            pltpu.VMEM((2, 2, width, width), F32),
            pltpu.VMEM((2, 2, width, width), F32),
            pltpu.VMEM((2, 2, 2, width, width), BF16),
            pltpu.VMEM((2, 2, 2, width, width), BF16),
            pltpu.VMEM((2, 2, width, width), F32),
            pltpu.VMEM((2, 2, width, width), F32),
            pltpu.VMEM((8, 2, half, width), F32),
            pltpu.VMEM((2, 4, width, width), BF16),
            pltpu.VMEM((2, 4, width, width), BF16),
            pltpu.SemaphoreType.DMA((20,)),
            pltpu.SemaphoreType.DMA((8,)),
            pltpu.SemaphoreType.DMA((9,)),
        ],
        cost_estimate=pl.CostEstimate(flops=8 * 48 * 2 * width**3, bytes_accessed=16 << 20, transcendentals=8 * width**2),
        name="slot_gradients",
    )(count, shifts, core, odd, own, row_a, row_b, side_in, side_out, ends_in, ends_out, probe, amps, mats, mats_t)


def edges_kernel(core_at, odd_at, slab_ref, in_ref, out_ref, a_ref, b_ref):
    core, odd = core_at[0], odd_at[0]
    for n, row in ((1 - odd, a_ref), (odd, b_ref)):
        for j, side in ((1 - core, in_ref), (core, out_ref)):
            row[j] = slab_ref[n, j] + side[n]


def merged_edges(core, odd, slabs, end_in, end_out):
    half = slabs.shape[-1]
    smem = pl.BlockSpec(memory_space=pltpu.SMEM)
    ends = pl.BlockSpec((2, 1, 2, half, half), lambda s: (0, s, 0, 0, 0))
    return pl.pallas_call(
        edges_kernel,
        grid=(2,),
        in_specs=[smem, smem, pl.BlockSpec((2, 2, 1, 2, half, half), lambda s: (0, 0, s, 0, 0, 0)), ends, ends],
        out_specs=[ends] * 2,
        out_shape=[jax.ShapeDtypeStruct(slabs.shape[1:], F32)] * 2,
        cost_estimate=pl.CostEstimate(flops=8 * 2 * half**2, bytes_accessed=3 << 20, transcendentals=0),
        compiler_params=pltpu.CompilerParams(vmem_limit_bytes=12 << 20),
        name="merge_edges",
    )(core, odd, slabs, end_in, end_out)


def core_kernel(core_at, odd_at, core_ref, in_ref, out_ref, a_ref, b_ref, grad_ref):
    half = in_ref.shape[-1]
    core, odd = core_at[0], odd_at[0]
    for h, row in ((1 - odd, a_ref), (odd, b_ref)):
        rows = pl.ds(pl.multiple_of(h * half, half), half)
        for j, side in ((1 - core, in_ref), (core, out_ref)):
            cols = pl.ds(pl.multiple_of(j * half, half), half)
            grad_ref[0, :, rows, cols] = core_ref[j, 0, :, rows, :] + side[0, :, rows, :] + row[j, 0]


def merged_core(core, odd, middle, side_in, side_out, row_a, row_b):
    width = middle.shape[3]
    half = width // 2
    smem = pl.BlockSpec(memory_space=pltpu.SMEM)
    side = pl.BlockSpec((1, 2, width, half), lambda s: (s, 0, 0, 0))
    rows = pl.BlockSpec((2, 1, 2, half, half), lambda s: (0, s, 0, 0, 0))
    return pl.pallas_call(
        core_kernel,
        grid=(2,),
        in_specs=[smem, smem, pl.BlockSpec((2, 1, 2, width, half), lambda s: (0, s, 0, 0, 0)), side, side, rows, rows],
        out_specs=pl.BlockSpec((1, 2, width, width), lambda s: (s, 0, 0, 0)),
        out_shape=jax.ShapeDtypeStruct((2, 2, width, width), F32),
        cost_estimate=pl.CostEstimate(flops=8 * width**2, bytes_accessed=4 << 20, transcendentals=0),
        compiler_params=pltpu.CompilerParams(vmem_limit_bytes=12 << 20),
        name="merge_core",
    )(core, odd, middle, side_in, side_out, row_a, row_b)


def swap(value, axis, first):
    pairs = [(n, n + 1) for n in range(first, lax.axis_size(axis) - 1, 2)]
    return lax.ppermute(value, axis, pairs + [(after, before) for before, after in pairs])


def total_over_devices(shard):
    planes, rows, cols = shard.shape
    blocks = shard.reshape(planes, rows // 8, 8, cols // 128, 128).swapaxes(2, 3).reshape(-1, 8, 128)
    parts = lax.all_to_all(blocks, ALL, 0, 0, tiled=True)
    mine = parts.sum(0, keepdims=True)
    whole = lax.all_to_all(jnp.broadcast_to(mine, parts.shape), ALL, 0, 0, tiled=True)
    return whole.reshape(planes, rows // 8, cols // 128, 8, 128).swapaxes(2, 3).reshape(shard.shape)


def by_column(rows):
    half = rows.shape[-1] // 2
    return jnp.stack([rows[..., :half], rows[..., half:]])


def shards(mats, mats_t, object_slices, probe, amplitudes, offsets, counts):
    half = probe.shape[-1] // 2
    core = lax.axis_index(TILE) % 2
    odd = lax.axis_index(POS) % 2
    by_core = (core.reshape(1), odd.reshape(1))

    def pick(where, when_zero, when_one):
        return jnp.where(where == 0, when_zero, when_one)

    top, bottom = by_column(object_slices[:, :, :half]), by_column(object_slices[:, :, half:])
    row_a = swap(pick(odd, bottom, top), POS, 0)
    row_b = swap(pick(odd, top, bottom), POS, 1)
    west, east = object_slices[..., :half], object_slices[..., half:]
    side_in = swap(pick(core, east, west), TILE, 0)
    side_out = swap(pick(core, west, east), TILE, 1)
    ends_out = swap(jnp.stack([pick(core, row_a[0], row_a[1]), pick(core, row_b[0], row_b[1])]), TILE, 1)
    ends_in = swap(jnp.stack([pick(core, row_a[1], row_a[0]), pick(core, row_b[1], row_b[0])]), TILE, 0)
    amps = ordered(amplitudes[0, 0])
    end_in, end_out, grad_in, grad_out, slabs, middle, probe_grad = gradients(
        counts, offsets[0, 0], *by_core, object_slices, row_a, row_b, side_in, side_out, ends_in, ends_out, probe, amps, mats, mats_t
    )
    end_out = swap(end_out, TILE, 1)
    end_in = swap(end_in, TILE, 0)
    grad_out = swap(grad_out, TILE, 1)
    grad_in = swap(grad_in, TILE, 0)
    probe_total = total_over_devices(probe_grad)
    row_a, row_b = merged_edges(*by_core, slabs, end_in, end_out)
    row_a = swap(row_a, POS, 0)
    row_b = swap(row_b, POS, 1)
    object_grad = merged_core(*by_core, middle, grad_in, grad_out, row_a, row_b)
    return (object_grad, probe_total)


def solution(mesh):
    torus = Mesh(mesh.devices.reshape(4, 4, 4, 2), ("pos_0", "pos_1", "tile_0", "tile_1"))
    placed = (
        P(None, None, POS, TILE),
        P(),
        P(POS, TILE, None, None, None),
        P(POS, TILE, None, None),
        P(POS, TILE),
    )
    real = transform_matrices(256)
    mats = jnp.asarray(halves(real))
    mats_t = jnp.asarray(halves(np.swapaxes(real, 1, 2)))
    return jax.shard_map(
        functools.partial(shards, mats, mats_t),
        mesh=torus,
        in_specs=placed,
        out_specs=(P(None, None, POS, TILE), P()),
        check_vma=False,
    )
```

profile of v0, /device:TPU:1, one launch (start us, length us, event | category | flops | bytes accessed | tf_op | source)
XLA Modules:
  0.0 114.5 jit_solution(14727764269331886246)
XLA Ops:
  0.7 1.4 %slice_bitcast_fusion.3 = (f32[1,2,2,128,128]{4,3,2,1,0:T(8,128)S(1)}, f32[1,2,2,128,128]{4,3,2,1,0:T(8,128)S(1)}, f32[1,2,2,128,128]{4,3,2,1,0:T(8,128)S(1)}, f32[1,2,2,128,128]{4,3,2,1,0:T(8,128)S(1)}) fusion(f32[2,2,256,256]{3,2,1,0:T(8,128)} %own_ref.1), kind=kLoop, calls=%fused_computation.11 | loop fusion | bytes 2097152 | tf_op jit(solution)/shard_map/stack | solution.py:439
  2.1 0.1 fusion
  2.2 1.5 %collective-permute-start.1 = (f32[2,2,2,128,128]{4,3,2,1,0:T(8,128)S(1)}, f32[2,2,2,128,128]{4,3,2,1,0:T(8,128)}, u32[]{:S(2)}, u32[]{:S(2)}) collective-permute-start(f32[2,2,2,128,128]{4,3,2,1,0:T(8,128)S(1)} %get-tuple-element.22), channel_id=1, source_target_pairs={{8,16},{24,32},{40,48},{56,64},{72,80},{88,96},{104,112},{16,8},{3... | collective-permute-start | bytes 1572872 | tf_op jit(solution)/shard_map/ppermute | solution.py:425
  3.6 4.6 %collective-permute-start = (f32[2,2,2,128,128]{4,3,2,1,0:T(8,128)S(1)}, f32[2,2,2,128,128]{4,3,2,1,0:T(8,128)}, u32[]{:S(2)}, u32[]{:S(2)}) collective-permute-start(f32[2,2,2,128,128]{4,3,2,1,0:T(8,128)S(1)} %get-tuple-element.23), channel_id=1, source_target_pairs={{0,8},{16,24},{32,40},{48,56},{64,72},{80,88},{96,104},{112,120},{... | collective-permute-start | bytes 1572872 | tf_op jit(solution)/shard_map/ppermute | solution.py:425
  8.2 0.1 slice_select_fusion
  8.3 4.2 %collective-permute-start.3 = (f32[2,2,256,128]{3,2,1,0:T(8,128)S(1)}, f32[2,2,256,128]{3,2,1,0:T(8,128)}, u32[]{:S(2)}, u32[]{:S(2)}) collective-permute-start(f32[2,2,256,128]{3,2,1,0:T(8,128)S(1)} %get-tuple-element.20), channel_id=1, source_target_pairs={{1,2},{3,4},{5,6},{2,1},{4,3},{6,5},{9,10},{11,12},{13,14},{10,9},... | collective-permute-start | bytes 1572872 | tf_op jit(solution)/shard_map/ppermute | solution.py:425
  12.6 0.0 copy-start.3
  12.6 0.1 collective-permute-start.2
  12.7 1.1 slice_select_fusion.2
  13.8 5.9 %collective-permute-done.row_a_ref = f32[2,2,2,128,128]{4,3,2,1,0:T(8,128)} collective-permute-done((f32[2,2,2,128,128]{4,3,2,1,0:T(8,128)S(1)}, f32[2,2,2,128,128]{4,3,2,1,0:T(8,128)}, u32[]{:S(2)}, u32[]{:S(2)}) %collective-permute-start) | collective-permute-done | bytes 524320 | tf_op jit(solution)/shard_map/ppermute | solution.py:425
  19.7 1.1 slice_select_fusion.4
  20.8 1.6 %collective-permute-start.4 = (f32[2,2,2,128,128]{4,3,2,1,0:T(8,128)S(1)}, f32[2,2,2,128,128]{4,3,2,1,0:T(8,128)S(1)}, u32[]{:S(2)}, u32[]{:S(2)}) collective-permute-start(f32[2,2,2,128,128]{4,3,2,1,0:T(8,128)S(1)} %pad_maximum_fusion.2), channel_id=1, source_target_pairs={{0,1},{2,3},{4,5},{6,7},{1,0},{3,2},{5,4},{7,6},{8,9},{10,11},{12,... | collective-permute-start | bytes 1572872 | tf_op jit(solution)/shard_map/ppermute | solution.py:425
  22.5 3.0 %collective-permute-start.5 = (f32[2,2,2,128,128]{4,3,2,1,0:T(8,128)S(1)}, f32[2,2,2,128,128]{4,3,2,1,0:T(8,128)S(1)}, u32[]{:S(2)}, u32[]{:S(2)}) collective-permute-start(f32[2,2,2,128,128]{4,3,2,1,0:T(8,128)S(1)} %pad_maximum_fusion.3), channel_id=1, source_target_pairs={{1,2},{3,4},{5,6},{2,1},{4,3},{6,5},{9,10},{11,12},{13,14},{10,9},... | collective-permute-start | bytes 1572872 | tf_op jit(solution)/shard_map/ppermute | solution.py:425
  26.2 0.7 copy.10.shift_ref
  26.8 6.8 %order_amps.1.amps_ref = f32[8,2,128,256]{3,2,1,0:T(8,128)} custom-call(f32[8,256,256]{2,1,0:T(8,128)} %bitcast.22, f32[8,256,256]{2,1,0:T(8,128)} %bitcast.23, bf16[256,256]{1,0:T(8,128)(2,1)} %constant.43.clone.perm_ref), custom_call_target="tpu_custom_call" | custom-call | flops 805306368 | bytes 4194304 | tf_op jit(solution)/shard_map/order_amps/pallas_call | solution.py:76
  33.7 0.8 copy-done.4
  34.5 0.2 copy-done.5
  34.7 13.1 %slot_gradients.1 = (f32[2,2,2,128,128]{4,3,2,1,0:T(8,128)}, f32[2,2,2,128,128]{4,3,2,1,0:T(8,128)}, f32[2,2,256,128]{3,2,1,0:T(8,128)}, f32[2,2,256,128]{3,2,1,...) custom-call(s32[1,1]{1,0:T(1,128)S(6)} %copy.12.count_ref, ...), custom_call_target="tpu_custom_call" | custom-call | flops 12884901888 | bytes 16777216 | tf_op jit(solution)/shard_map/slot_gradients/pallas_call | solution.py:346
  47.8 2.9 %collective-permute-start.8 = (f32[2,2,2,128,128]{4,3,2,1,0:T(8,128)}, f32[2,2,2,128,128]{4,3,2,1,0:T(8,128)S(1)}, u32[]{:S(2)}, u32[]{:S(2)}) collective-permute-start(f32[2,2,2,128,128]{4,3,2,1,0:T(8,128)} %get-tuple-element.15), channel_id=1, source_target_pairs={{0,1},{2,3},{4,5},{6,7},{1,0},{3,2},{5,4},{7,6},{8,9},{10,11},{12,... | collective-permute-start | bytes 1572872 | tf_op jit(solution)/shard_map/ppermute | solution.py:425
  50.6 4.9 %collective-permute-start.9 = (f32[2,2,2,128,128]{4,3,2,1,0:T(8,128)}, f32[2,2,2,128,128]{4,3,2,1,0:T(8,128)S(1)}, u32[]{:S(2)}, u32[]{:S(2)}) collective-permute-start(f32[2,2,2,128,128]{4,3,2,1,0:T(8,128)} %get-tuple-element.16), channel_id=1, source_target_pairs={{1,2},{3,4},{5,6},{2,1},{4,3},{6,5},{9,10},{11,12},{13,14},{10,9},... | collective-permute-start | bytes 1572872 | tf_op jit(solution)/shard_map/ppermute | solution.py:425
  55.6 23.3 %all-to-all-start = ((f32[128,8,128]{2,1,0:T(8,128)}), f32[128,8,128]{2,1,0:T(8,128)}, u32[]{:S(2)}, u32[]{:S(2)}) async-start(f32[128,8,128]{2,1,0:T(8,128)} %bitcast.25), calls=%async_computation | async-start | bytes 1048576 | tf_op jit(solution)/shard_map/all_to_all | solution.py:431
  78.8 1.2 %collective-permute-start.6 = (f32[2,2,256,128]{3,2,1,0:T(8,128)}, f32[2,2,256,128]{3,2,1,0:T(8,128)S(1)}, u32[]{:S(2)}, u32[]{:S(2)}) collective-permute-start(f32[2,2,256,128]{3,2,1,0:T(8,128)} %get-tuple-element.12), channel_id=1, source_target_pairs={{0,1},{2,3},{4,5},{6,7},{1,0},{3,2},{5,4},{7,6},{8,9},{10,11},{12,... | collective-permute-start | bytes 1572872 | tf_op jit(solution)/shard_map/ppermute | solution.py:425
  80.0 2.5 %collective-permute-start.7 = (f32[2,2,256,128]{3,2,1,0:T(8,128)}, f32[2,2,256,128]{3,2,1,0:T(8,128)S(1)}, u32[]{:S(2)}, u32[]{:S(2)}) collective-permute-start(f32[2,2,256,128]{3,2,1,0:T(8,128)} %get-tuple-element.13), channel_id=1, source_target_pairs={{1,2},{3,4},{5,6},{2,1},{4,3},{6,5},{9,10},{11,12},{13,14},{10,9},... | collective-permute-start | bytes 1572872 | tf_op jit(solution)/shard_map/ppermute | solution.py:425
  82.6 1.2 %copy-done.1 = f32[2,2,2,2,128,128]{5,4,3,2,1,0:T(8,128)S(1)} copy-done((f32[2,2,2,2,128,128]{5,4,3,2,1,0:T(8,128)S(1)}, f32[2,2,2,2,128,128]{5,4,3,2,1,0:T(8,128)}, u32[]{:S(2)}) %copy-start.1) | copy-done | bytes 1048600
  83.8 1.2 %merge_edges.1 = (f32[2,2,2,128,128]{4,3,2,1,0:T(8,128)}, f32[2,2,2,128,128]{4,3,2,1,0:T(8,128)}) custom-call(s32[1]{0:T(128)} %bitcast.core_at, s32[1]{0:T(128)} %bitcast.1.odd_at, f32[2,2,2,2,128,128]{5,4,3,2,1,0:T(8,128)S(1)} %copy-done.1, f32[2,2,2,128,128]{4,3,2,1,0:T(8,128)S(1)} %collective-permute-done.8.in_ref, ...), custom_call_target="tpu_custom_call" | custom-call | flops 262144 | bytes 3145728 | tf_op jit(solution)/shard_map/merge_edges/pallas_call | solution.py:383
  85.0 1.3 %collective-permute-start.10 = (f32[2,2,2,128,128]{4,3,2,1,0:T(8,128)}, f32[2,2,2,128,128]{4,3,2,1,0:T(8,128)S(1)}, u32[]{:S(2)}, u32[]{:S(2)}) collective-permute-start(f32[2,2,2,128,128]{4,3,2,1,0:T(8,128)} %get-tuple-element.17), channel_id=1, source_target_pairs={{0,8},{16,24},{32,40},{48,56},{64,72},{80,88},{96,104},{112,120},{... | collective-permute-start | bytes 1572872 | tf_op jit(solution)/shard_map/ppermute | solution.py:425
  86.3 0.7 collective-permute-start.11
  87.0 5.1 %all-to-all-done = f32[128,8,128]{2,1,0:T(8,128)} async-done(((f32[128,8,128]{2,1,0:T(8,128)}), f32[128,8,128]{2,1,0:T(8,128)}, u32[]{:S(2)}, u32[]{:S(2)}) %all-to-all-start) | async-done | bytes 524320 | tf_op jit(solution)/shard_map/all_to_all | solution.py:431
  92.1 1.2 %reduce_sum.9 = f32[8,128]{1,0:T(8,128)S(1)} reduce(f32[128,8,128]{2,1,0:T(8,128)} %all-to-all-done, f32[]{:T(128)} %constant.42.clone.1), dimensions={0}, to_apply=%region_0.1 | reduce | flops 130048 | bytes 528388 | tf_op jit(solution)/shard_map/reduce_sum | solution.py:432
  93.3 19.1 %all_to_all.10 = f32[128,8,128]{2,1,0:T(8,128)S(1)} all-to-all(f32[128,8,128]{2,1,0:T(8,128)S(1)} %broadcast_in_dim.2), channel_id=1, replica_groups=mesh['pos_0'=4,'pos_1'=4,'tile_0'=4,'tile_1'=2] {'pos_0','pos_1','tile_0..., dimensions={0} | all-to-all | bytes 1048576 | tf_op jit(solution)/shard_map/all_to_all | solution.py:433
  112.4 1.3 %merge_core.1 = f32[2,2,256,256]{3,2,1,0:T(8,128)} custom-call(s32[1]{0:T(128)} %bitcast.core_at, s32[1]{0:T(128)} %bitcast.1.odd_at, f32[2,2,2,256,128]{4,3,2,1,0:T(8,128)S(1)} %copy-done, f32[2,2,256,128]{3,2,1,0:T(8,128)S(1)} %collective-permute-done.6.in_ref, f32[2,2,256,128]{3,2,1,0:T(8,128)S(1)} %collective-permute-done.7.out_ref, ...), custom_call_target="tpu_custom_call" | custom-call | flops 524288 | bytes 4194304 | tf_op jit(solution)/shard_map/merge_core/pallas_call | solution.py:411
  113.7 0.8 copy.13
  (22 shorter events, 0.2 us)
Async XLA Ops:
  0.6 7.6 %copy-start.2 = (f32[2,2,256,256]{3,2,1,0:T(8,128)S(1)}, f32[2,2,256,256]{3,2,1,0:T(8,128)}, u32[]{:S(2)}) copy-start(f32[2,2,256,256]{3,2,1,0:T(8,128)} %own_ref.1) | copy-start | bytes 3145732
  2.2 10.5 %collective-permute-start.1 = (f32[2,2,2,128,128]{4,3,2,1,0:T(8,128)S(1)}, f32[2,2,2,128,128]{4,3,2,1,0:T(8,128)}, u32[]{:S(2)}, u32[]{:S(2)}) collective-permute-start(f32[2,2,2,128,128]{4,3,2,1,0:T(8,128)S(1)} %get-tuple-element.22), channel_id=1, source_target_pairs={{8,16},{24,32},{40,48},{56,64},{72,80},{88,96},{104,112},{16,8},{3... | collective-permute-start | bytes 1572872 | tf_op jit(solution)/shard_map/ppermute | solution.py:425
  3.6 16.1 %collective-permute-start = (f32[2,2,2,128,128]{4,3,2,1,0:T(8,128)S(1)}, f32[2,2,2,128,128]{4,3,2,1,0:T(8,128)}, u32[]{:S(2)}, u32[]{:S(2)}) collective-permute-start(f32[2,2,2,128,128]{4,3,2,1,0:T(8,128)S(1)} %get-tuple-element.23), channel_id=1, source_target_pairs={{0,8},{16,24},{32,40},{48,56},{64,72},{80,88},{96,104},{112,120},{... | collective-permute-start | bytes 1572872 | tf_op jit(solution)/shard_map/ppermute | solution.py:425
  8.3 25.3 %collective-permute-start.3 = (f32[2,2,256,128]{3,2,1,0:T(8,128)S(1)}, f32[2,2,256,128]{3,2,1,0:T(8,128)}, u32[]{:S(2)}, u32[]{:S(2)}) collective-permute-start(f32[2,2,256,128]{3,2,1,0:T(8,128)S(1)} %get-tuple-element.20), channel_id=1, source_target_pairs={{1,2},{3,4},{5,6},{2,1},{4,3},{6,5},{9,10},{11,12},{13,14},{10,9},... | collective-permute-start | bytes 1572872 | tf_op jit(solution)/shard_map/ppermute | solution.py:425
  12.6 13.6 %copy-start.3 = (s32[1,1,8,2]{2,3,1,0:T(2,128)S(1)}, s32[1,1,8,2]{2,3,1,0:T(2,128)}, u32[]{:S(2)}) copy-start(s32[1,1,8,2]{2,3,1,0:T(2,128)} %param.11) | copy-start | bytes 196
  12.6 21.1 %collective-permute-start.2 = (f32[2,2,256,128]{3,2,1,0:T(8,128)S(1)}, f32[2,2,256,128]{3,2,1,0:T(8,128)}, u32[]{:S(2)}, u32[]{:S(2)}) collective-permute-start(f32[2,2,256,128]{3,2,1,0:T(8,128)S(1)} %get-tuple-element.21), channel_id=1, source_target_pairs={{0,1},{2,3},{4,5},{6,7},{1,0},{3,2},{5,4},{7,6},{8,9},{10,11},{12,... | collective-permute-start | bytes 1572872 | tf_op jit(solution)/shard_map/ppermute | solution.py:425
  20.8 12.8 %collective-permute-start.4 = (f32[2,2,2,128,128]{4,3,2,1,0:T(8,128)S(1)}, f32[2,2,2,128,128]{4,3,2,1,0:T(8,128)S(1)}, u32[]{:S(2)}, u32[]{:S(2)}) collective-permute-start(f32[2,2,2,128,128]{4,3,2,1,0:T(8,128)S(1)} %pad_maximum_fusion.2), channel_id=1, source_target_pairs={{0,1},{2,3},{4,5},{6,7},{1,0},{3,2},{5,4},{7,6},{8,9},{10,11},{12,... | collective-permute-start | bytes 1572872 | tf_op jit(solution)/shard_map/ppermute | solution.py:425
  22.5 11.2 %collective-permute-start.5 = (f32[2,2,2,128,128]{4,3,2,1,0:T(8,128)S(1)}, f32[2,2,2,128,128]{4,3,2,1,0:T(8,128)S(1)}, u32[]{:S(2)}, u32[]{:S(2)}) collective-permute-start(f32[2,2,2,128,128]{4,3,2,1,0:T(8,128)S(1)} %pad_maximum_fusion.3), channel_id=1, source_target_pairs={{1,2},{3,4},{5,6},{2,1},{4,3},{6,5},{9,10},{11,12},{13,14},{10,9},... | collective-permute-start | bytes 1572872 | tf_op jit(solution)/shard_map/ppermute | solution.py:425
  33.7 0.8 copy-start.4
  33.7 1.0 copy-start.5
  47.8 34.8 %collective-permute-start.8 = (f32[2,2,2,128,128]{4,3,2,1,0:T(8,128)}, f32[2,2,2,128,128]{4,3,2,1,0:T(8,128)S(1)}, u32[]{:S(2)}, u32[]{:S(2)}) collective-permute-start(f32[2,2,2,128,128]{4,3,2,1,0:T(8,128)} %get-tuple-element.15), channel_id=1, source_target_pairs={{0,1},{2,3},{4,5},{6,7},{1,0},{3,2},{5,4},{7,6},{8,9},{10,11},{12,... | collective-permute-start | bytes 1572872 | tf_op jit(solution)/shard_map/ppermute | solution.py:425
  50.6 32.0 %collective-permute-start.9 = (f32[2,2,2,128,128]{4,3,2,1,0:T(8,128)}, f32[2,2,2,128,128]{4,3,2,1,0:T(8,128)S(1)}, u32[]{:S(2)}, u32[]{:S(2)}) collective-permute-start(f32[2,2,2,128,128]{4,3,2,1,0:T(8,128)} %get-tuple-element.16), channel_id=1, source_target_pairs={{1,2},{3,4},{5,6},{2,1},{4,3},{6,5},{9,10},{11,12},{13,14},{10,9},... | collective-permute-start | bytes 1572872 | tf_op jit(solution)/shard_map/ppermute | solution.py:425
  55.6 36.5 %all-to-all-start = ((f32[128,8,128]{2,1,0:T(8,128)}), f32[128,8,128]{2,1,0:T(8,128)}, u32[]{:S(2)}, u32[]{:S(2)}) async-start(f32[128,8,128]{2,1,0:T(8,128)} %bitcast.25), calls=%async_computation | async-start | bytes 1048576 | tf_op jit(solution)/shard_map/all_to_all | solution.py:431
  78.8 33.6 %collective-permute-start.6 = (f32[2,2,256,128]{3,2,1,0:T(8,128)}, f32[2,2,256,128]{3,2,1,0:T(8,128)S(1)}, u32[]{:S(2)}, u32[]{:S(2)}) collective-permute-start(f32[2,2,256,128]{3,2,1,0:T(8,128)} %get-tuple-element.12), channel_id=1, source_target_pairs={{0,1},{2,3},{4,5},{6,7},{1,0},{3,2},{5,4},{7,6},{8,9},{10,11},{12,... | collective-permute-start | bytes 1572872 | tf_op jit(solution)/shard_map/ppermute | solution.py:425
  80.0 32.3 %collective-permute-start.7 = (f32[2,2,256,128]{3,2,1,0:T(8,128)}, f32[2,2,256,128]{3,2,1,0:T(8,128)S(1)}, u32[]{:S(2)}, u32[]{:S(2)}) collective-permute-start(f32[2,2,256,128]{3,2,1,0:T(8,128)} %get-tuple-element.13), channel_id=1, source_target_pairs={{1,2},{3,4},{5,6},{2,1},{4,3},{6,5},{9,10},{11,12},{13,14},{10,9},... | collective-permute-start | bytes 1572872 | tf_op jit(solution)/shard_map/ppermute | solution.py:425
  82.6 1.2 %copy-start.1 = (f32[2,2,2,2,128,128]{5,4,3,2,1,0:T(8,128)S(1)}, f32[2,2,2,2,128,128]{5,4,3,2,1,0:T(8,128)}, u32[]{:S(2)}) copy-start(f32[2,2,2,2,128,128]{5,4,3,2,1,0:T(8,128)} %get-tuple-element.14.slab_ref) | copy-start | bytes 3145732
  83.8 28.6 %copy-start = (f32[2,2,2,256,128]{4,3,2,1,0:T(8,128)S(1)}, f32[2,2,2,256,128]{4,3,2,1,0:T(8,128)}, u32[]{:S(2)}) copy-start(f32[2,2,2,256,128]{4,3,2,1,0:T(8,128)} %get-tuple-element.11.core_ref) | copy-start | bytes 3145732
  85.0 27.4 %collective-permute-start.10 = (f32[2,2,2,128,128]{4,3,2,1,0:T(8,128)}, f32[2,2,2,128,128]{4,3,2,1,0:T(8,128)S(1)}, u32[]{:S(2)}, u32[]{:S(2)}) collective-permute-start(f32[2,2,2,128,128]{4,3,2,1,0:T(8,128)} %get-tuple-element.17), channel_id=1, source_target_pairs={{0,8},{16,24},{32,40},{48,56},{64,72},{80,88},{96,104},{112,120},{... | collective-permute-start | bytes 1572872 | tf_op jit(solution)/shard_map/ppermute | solution.py:425
  86.3 26.1 %collective-permute-start.11 = (f32[2,2,2,128,128]{4,3,2,1,0:T(8,128)}, f32[2,2,2,128,128]{4,3,2,1,0:T(8,128)S(1)}, u32[]{:S(2)}, u32[]{:S(2)}) collective-permute-start(f32[2,2,2,128,128]{4,3,2,1,0:T(8,128)} %get-tuple-element.18), channel_id=1, source_target_pairs={{8,16},{24,32},{40,48},{56,64},{72,80},{88,96},{104,112},{16,8},{3... | collective-permute-start | bytes 1572872 | tf_op jit(solution)/shard_map/ppermute | solution.py:425
where the time goes:
time: 115 us; the launch traced here: 114 us
  starting transfers between devices  51.8 us (45%)
  Pallas kernels  22.3 us (19%)
  blocking collectives  19.1 us (17%)
  waiting for transfers between devices  11 us (10%)
  local copies, waits for them, and re-layouts  5.12 us (4%)
  other arithmetic  3.54 us (3%)
  between operations  1.53 us (1%)
    ppermute x12, starting transfers between devices, swap(): lax.ppermute(value, axis, pairs + [(after, before) for before, after in p...  28.6 us
    all_to_all x1, starting transfers between devices, total_over_devices(): parts = lax.all_to_all(blocks, ALL, 0, 0, tiled=True)  23.3 us
    all_to_all x1, blocking collectives, total_over_devices(): lax.all_to_all(jnp.broadcast_to(mine, parts.shape), ALL, 0, 0, tiled=True)  19.1 us
    pallas_call x1, Pallas kernels, gradients(): pl.pallas_call(main_kernel, in_specs=[smem] * 4 + [any_space] * 7 + [vmem...  13.1 us
    pallas_call x1, Pallas kernels, ordered(): pl.pallas_call(order_kernel, grid=(slots,), in_specs=[pl.BlockSpec((1, wi...  6.81 us
    ppermute x12, waiting for transfers between devices, swap(): lax.ppermute(value, axis, pairs + [(after, before) for before, after in p...  5.96 us
    all_to_all x1, waiting for transfers between devices, total_over_devices(): parts = lax.all_to_all(blocks, ALL, 0, 0, tiled=True)  5.06 us
    unnamed x13, local copies, waits for them, and re-layouts  3.01 us
  transfers between devices with their start and end apart: 13, of which 2 were waited for; matrix products, arithmetic and copies ran while one was open for 4% of the time, Pallas kernels for 7%

commit v1 on v0

--- a/solution.py
+++ b/solution.py
@@ -55,76 +55,67 @@
     return jnp.dot(left, right, preferred_element_type=F32)
 
 
-def order_kernel(left_ref, right_ref, perm_ref, out_ref):
-    half = left_ref.shape[1] // 2
-    for parity in range(2):
-        picked = pl.ds(parity, half, stride=2)
-        rows = jnp.concatenate([left_ref[0, picked, :], right_ref[0, picked, :]], axis=1)
-        first = rows.astype(BF16)
-        rest = rows - first.astype(F32)
-        second = rest.astype(BF16)
-        third = (rest - second.astype(F32)).astype(BF16)
-        perm = perm_ref[...]
-        out_ref[0, parity] = dot(first, perm) + dot(second, perm) + dot(third, perm)
-
-
-def ordered(amps):
-    slots, width, _ = amps.shape
+def even_then_odd(width):
     index = np.arange(width)
     source = np.where(index < width // 2, 2 * index, 2 * (index - width // 2) + 1)
-    perm = (index[:, None] == source[None, :]).astype(BF16)
-    return pl.pallas_call(
-        order_kernel,
-        grid=(slots,),
-        in_specs=[
-            pl.BlockSpec((1, width, width // 2), lambda i: (i, 0, 0)),
-            pl.BlockSpec((1, width, width // 2), lambda i: (i, 0, 1)),
-            pl.BlockSpec((width, width), lambda i: (0, 0)),
-        ],
-        out_specs=pl.BlockSpec((1, 2, width // 2, width), lambda i: (i, 0, 0, 0)),
-        out_shape=jax.ShapeDtypeStruct((slots, 2, width // 2, width), F32),
-        cost_estimate=pl.CostEstimate(flops=2 * 3 * slots * width**3, bytes_accessed=8 * slots * width**2, transcendentals=0),
-        name="order_amps",
-    )(amps, amps, jnp.asarray(perm))
+    return (index[:, None] == source[None, :]).astype(BF16)
 
 
 def main_kernel(
-    count_ref, shift_ref, core_at, odd_at, own_ref, row_a_ref, row_b_ref, in_ref, out_ref, in_ends_ref, out_ends_ref, probe_ref, amps_ref, mats_ref, matts_ref,
-    end_in_ref, end_out_ref, side_in_ref, side_out_ref, slab_ref, core_ref, probe_grad_ref,
-    ext, gext, rolleds, waves, xas, was, vvs, zzs, amp_ref, mat_ref, matt_ref, sems, amp_sems, out_sems,
+    count_ref, shift_ref, core_at, odd_at, own_ref, out_a_ref, out_b_ref, in_a_ref, in_b_ref, side_in_ref, side_out_ref,
+    end_in_a_ref, end_in_b_ref, end_out_a_ref, end_out_b_ref, probe_hbm, amps_ref, mats_ref, matts_ref, perms_ref,
+    grad_end_in, grad_end_out, grad_side_in, grad_side_out, slab_ref, core_ref, probe_grad_hbm,
+    ext, gext, probe_ref, probe_grad_ref, rolleds, waves, xas, was, vvs, zzs, aas, aps, amp_ref, mat_ref, matt_ref, perm_ref, sems, amp_sems, out_sems,
 ):
     half = 128
     grads = [gext.at[j] for j in range(4)]
-    copies = []
-    for s in range(2):
-        for c in range(2):
-            for j in range(2):
-                copies.append((own_ref.at[s, c, :, pl.ds(j * half, half)], ext.at[1 + j, s, c, pl.ds(half, 2 * half), :]))
     middle = pl.ds(half, 2 * half)
     core, odd = core_at[0], odd_at[0]
     toward_in, toward_out = 3 * (1 - core), 3 * core
     rows_a = pl.ds(pl.multiple_of(3 * half * (1 - odd), half), half)
     rows_b = pl.ds(pl.multiple_of(3 * half * odd, half), half)
-    copies.append((row_a_ref, ext.at[1:3, :, :, rows_a, :]))
-    copies.append((row_b_ref, ext.at[1:3, :, :, rows_b, :]))
-    for j, side, ends in ((toward_in, in_ref, in_ends_ref), (toward_out, out_ref, out_ends_ref)):
-        copies.append((side, ext.at[j, :, :, middle, :]))
-        copies.append((ends.at[0], ext.at[j, :, :, rows_a, :]))
-        copies.append((ends.at[1], ext.at[j, :, :, rows_b, :]))
-    copies = [pltpu.make_async_copy(a, b, sems.at[n]) for n, (a, b) in enumerate(copies)]
-    copies.append(pltpu.make_async_copy(mats_ref, mat_ref, sems.at[len(copies)]))
-    copies.append(pltpu.make_async_copy(matts_ref, matt_ref, sems.at[len(copies)]))
+
+    def slice_copies(s):
+        pairs = []
+        for c in range(2):
+            for j in range(2):
+                pairs.append((own_ref.at[s, c, :, pl.ds(j * half, half)], ext.at[1 + j, s, c, middle, :]))
+        for j, side, ends in (
+            (toward_in, side_in_ref, (end_in_a_ref, end_in_b_ref)),
+            (toward_out, side_out_ref, (end_out_a_ref, end_out_b_ref)),
+            (2 - core, None, (in_a_ref, in_b_ref)),
+            (1 + core, None, (out_a_ref, out_b_ref)),
+        ):
+            if side is not None:
+                pairs.append((side.at[s], ext.at[j, s, :, middle, :]))
+            pairs.append((ends[0].at[s], ext.at[j, s, :, rows_a, :]))
+            pairs.append((ends[1].at[s], ext.at[j, s, :, rows_b, :]))
+        return pairs
+
+    early = slice_copies(0) + [(probe_hbm, probe_ref)]
+    late = [(mats_ref, mat_ref), (matts_ref, matt_ref), (perms_ref, perm_ref)] + slice_copies(1)
+    copies = [pltpu.make_async_copy(a, b, sems.at[n]) for n, (a, b) in enumerate(early + late)]
     for copy in copies:
         copy.start()
 
-    def amp_copy(slot):
-        return pltpu.make_async_copy(amps_ref.at[slot], amp_ref.at[slot], amp_sems.at[slot])
+    def amp_copies(slot):
+        return [
+            pltpu.make_async_copy(
+                amps_ref.at[slot, :, pl.ds(j * half, half)], amp_ref.at[slot, j], amp_sems.at[slot, j]
+            )
+            for j in range(2)
+        ]
+
+    def wait_amps(slot):
+        for copy in amp_copies(slot):
+            copy.wait()
 
     for slot in range(8):
-        amp_copy(slot).start()
+        for copy in amp_copies(slot):
+            copy.start()
     gext[...] = jnp.zeros_like(gext)
     probe_grad_ref[...] = jnp.zeros_like(probe_grad_ref)
-    for copy in copies:
+    for copy in copies[: len(early)]:
         copy.wait()
 
     lane = lax.broadcasted_iota(jnp.int32, (ROWS, half), 1)
@@ -132,9 +123,10 @@
     count = count_ref[0, 0]
 
     def phases(which, slot, two):
-        rolled, wave, xa, wa, vv, zz = (ref.at[which] for ref in (rolleds, waves, xas, was, vvs, zzs))
-        top = shift_ref[slot, 0] + half
-        left = shift_ref[slot, 1] + half
+        refs = (rolleds, waves, xas, was, vvs, zzs, aas, aps)
+        rolled, wave, xa, wa, vv, zz, aa, ap = (ref.at[which] for ref in refs)
+        top = shift_ref[0, slot] + half
+        left = shift_ref[1, slot] + half
         back = lax.rem(2 * half - left, 2 * half)
         masks = (lane >= left, lane + half >= left)
 
@@ -205,6 +197,13 @@
             put(wa, 1, c * half + r, tiles[0], dif_s + dif_d)
             put(wa, 1, c * half + r, tiles[1], dif_s - dif_d)
 
+        def split_amps(k, r):
+            for j in range(2):
+                put(aa, k, r, tiles[j], amp_ref[slot, j, pl.ds(2 * r + k, ROWS, stride=2), :])
+
+        def order_amps(k):
+            ap[k] = dot(aa[0, k], perm_ref[...]) + dot(aa[1, k], perm_ref[...])
+
         def exit_wave(h, r):
             row = h * half + r
             pair = []
@@ -227,7 +226,7 @@
             for j in range(2):
                 fr = zz[k, pl.ds(r, ROWS), tiles[j]]
                 fi = zz[k, pl.ds(half + r, ROWS), tiles[j]]
-                a = amp_ref[slot, k, pl.ds(r, ROWS), tiles[j]]
+                a = ap[k, pl.ds(r, ROWS), tiles[j]]
                 factor = two - two * a * lax.rsqrt(fr * fr + fi * fi + 0.01)
                 put(wa, k, r, tiles[j], factor * fr)
                 put(wa, k, half + r, tiles[j], factor * fi)
@@ -276,8 +275,8 @@
             left_side(matt_ref, 0),
             over(exit_wave, pair, upper),
             right(mat_ref, 2),
-            over(turn_far, upper, pair),
-            left_side(matt_ref, 2),
+            over(turn_far, upper, pair) + over(split_amps, pair, upper),
+            left_side(matt_ref, 2) + over(order_amps, pair),
             over(compare, pair, upper),
             left_side(mat_ref, 2),
             over(turn_back, pair, upper),
@@ -291,25 +290,26 @@
 
     def visit(step, carry):
         first = 2 * step
-        amp_copy(first).wait()
-        amp_copy(first + 1).wait()
+        wait_amps(first)
+        wait_amps(first + 1)
         live = jnp.where(first + 1 < count, 2.0, 0.0)
         one = phases(0, first, 2.0)
         other = phases(1, jnp.minimum(first + 1, count - 1), live)
-        for run in one[0]:
-            run()
-        for ahead, behind in zip(one[1:], other[:-1]):
+        following = phases(0, jnp.minimum(first + 2, count - 1), 2.0)
+        for ahead, behind in zip(one[1:] + following[:1], other):
             interleave(ahead, behind)
-        for run in other[-1]:
-            run()
         return carry
 
+    for run in phases(0, 0, 2.0)[0]:
+        run()
+    for copy in copies[len(early) :]:
+        copy.wait()
     steps = lax.div(count + 1, 2)
     lax.fori_loop(0, steps, visit, 0)
 
     outer = (pl.ds(0, half), pl.ds(3 * half, half))
-    moves = [(gext.at[1:3, :, :, middle, :], core_ref)]
-    for j, end, side in ((toward_in, end_in_ref, side_in_ref), (toward_out, end_out_ref, side_out_ref)):
+    moves = [(gext.at[1:3, :, :, middle, :], core_ref), (probe_grad_ref, probe_grad_hbm)]
+    for j, end, side in ((toward_in, grad_end_in, grad_side_in), (toward_out, grad_end_out, grad_side_out)):
         moves.append((gext.at[j, :, :, middle, :], side))
         for n in range(2):
             moves.append((gext.at[j, :, :, outer[n], :], end.at[n]))
@@ -320,7 +320,7 @@
         move.start()
 
     def leave(slot, carry):
-        amp_copy(slot).wait()
+        wait_amps(slot)
         return carry
 
     lax.fori_loop(2 * steps, 8, leave, 0)
@@ -335,38 +335,42 @@
         (first, second)[which][n]()
 
 
-def gradients(count, shifts, core, odd, own, row_a, row_b, side_in, side_out, ends_in, ends_out, probe, amps, mats, mats_t):
-    width = probe.shape[-1]
+def gradients(count, shifts, core, odd, *arrays):
+    width = arrays[0].shape[-1]
     half = width // 2
     shapes = [(2, 2, 2, half, half)] * 2 + [(2, 2, width, half)] * 2 + [(2, 2, 2, 2, half, half), (2, 2, 2, width, half)]
     shapes.append((2, width, width))
     any_space = pl.BlockSpec(memory_space=pl.ANY)
-    vmem = pl.BlockSpec(memory_space=pltpu.VMEM)
     smem = pl.BlockSpec(memory_space=pltpu.SMEM)
     return pl.pallas_call(
         main_kernel,
-        in_specs=[smem] * 4 + [any_space] * 7 + [vmem] + [any_space] * 3,
-        out_specs=[any_space] * 6 + [vmem],
+        in_specs=[smem] * 4 + [any_space] * 16,
+        out_specs=[any_space] * 7,
         out_shape=[jax.ShapeDtypeStruct(shape, F32) for shape in shapes],
         scratch_shapes=[
             pltpu.VMEM((4, 2, 2, 4 * half, half), F32),
             pltpu.VMEM((4, 2, 2, 4 * half, half), F32),
+            pltpu.VMEM((2, width, width), F32),
+            pltpu.VMEM((2, width, width), F32),
             pltpu.VMEM((2, 2, width, width), F32),
             pltpu.VMEM((2, 2, width, width), F32),
             pltpu.VMEM((2, 2, 2, width, width), BF16),
             pltpu.VMEM((2, 2, 2, width, width), BF16),
             pltpu.VMEM((2, 2, width, width), F32),
             pltpu.VMEM((2, 2, width, width), F32),
-            pltpu.VMEM((8, 2, half, width), F32),
+            pltpu.VMEM((2, 2, 2, half, width), BF16),
+            pltpu.VMEM((2, 2, half, width), F32),
+            pltpu.VMEM((8, 2, width, half), F32),
             pltpu.VMEM((2, 4, width, width), BF16),
             pltpu.VMEM((2, 4, width, width), BF16),
-            pltpu.SemaphoreType.DMA((20,)),
-            pltpu.SemaphoreType.DMA((8,)),
-            pltpu.SemaphoreType.DMA((9,)),
+            pltpu.VMEM((width, width), BF16),
+            pltpu.SemaphoreType.DMA((32,)),
+            pltpu.SemaphoreType.DMA((8, 2)),
+            pltpu.SemaphoreType.DMA((10,)),
         ],
         cost_estimate=pl.CostEstimate(flops=8 * 48 * 2 * width**3, bytes_accessed=16 << 20, transcendentals=8 * width**2),
         name="slot_gradients",
-    )(count, shifts, core, odd, own, row_a, row_b, side_in, side_out, ends_in, ends_out, probe, amps, mats, mats_t)
+    )(count, shifts, core, odd, *arrays)
 
 
 def edges_kernel(core_at, odd_at, slab_ref, in_ref, out_ref, a_ref, b_ref):
@@ -392,7 +396,8 @@
     )(core, odd, slabs, end_in, end_out)
 
 
-def core_kernel(core_at, odd_at, core_ref, in_ref, out_ref, a_ref, b_ref, grad_ref):
+def core_kernel(core_at, odd_at, core_ref, in_ref, out_ref, a_ref, b_ref, total_ref, grad_ref, probe_ref):
+    probe_ref[...] = total_ref[...]
     half = in_ref.shape[-1]
     core, odd = core_at[0], odd_at[0]
     for h, row in ((1 - odd, a_ref), (odd, b_ref)):
@@ -402,22 +407,23 @@
             grad_ref[0, :, rows, cols] = core_ref[j, 0, :, rows, :] + side[0, :, rows, :] + row[j, 0]
 
 
-def merged_core(core, odd, middle, side_in, side_out, row_a, row_b):
+def merged_core(core, odd, middle, side_in, side_out, row_a, row_b, total):
     width = middle.shape[3]
     half = width // 2
     smem = pl.BlockSpec(memory_space=pltpu.SMEM)
     side = pl.BlockSpec((1, 2, width, half), lambda s: (s, 0, 0, 0))
     rows = pl.BlockSpec((2, 1, 2, half, half), lambda s: (0, s, 0, 0, 0))
+    plane = pl.BlockSpec((1, width, width), lambda s: (s, 0, 0))
     return pl.pallas_call(
         core_kernel,
         grid=(2,),
-        in_specs=[smem, smem, pl.BlockSpec((2, 1, 2, width, half), lambda s: (0, s, 0, 0, 0)), side, side, rows, rows],
-        out_specs=pl.BlockSpec((1, 2, width, width), lambda s: (s, 0, 0, 0)),
-        out_shape=jax.ShapeDtypeStruct((2, 2, width, width), F32),
+        in_specs=[smem, smem, pl.BlockSpec((2, 1, 2, width, half), lambda s: (0, s, 0, 0, 0)), side, side, rows, rows, plane],
+        out_specs=[pl.BlockSpec((1, 2, width, width), lambda s: (s, 0, 0, 0)), plane],
+        out_shape=[jax.ShapeDtypeStruct((2, 2, width, width), F32), jax.ShapeDtypeStruct(total.shape, F32)],
         cost_estimate=pl.CostEstimate(flops=8 * width**2, bytes_accessed=4 << 20, transcendentals=0),
         compiler_params=pltpu.CompilerParams(vmem_limit_bytes=12 << 20),
         name="merge_core",
-    )(core, odd, middle, side_in, side_out, row_a, row_b)
+    )(core, odd, middle, side_in, side_out, row_a, row_b, total)
 
 
 def swap(value, axis, first):
@@ -434,12 +440,7 @@
     return whole.reshape(planes, rows // 8, cols // 128, 8, 128).swapaxes(2, 3).reshape(shard.shape)
 
 
-def by_column(rows):
-    half = rows.shape[-1] // 2
-    return jnp.stack([rows[..., :half], rows[..., half:]])
-
-
-def shards(mats, mats_t, object_slices, probe, amplitudes, offsets, counts):
+def shards(mats, mats_t, perm, object_slices, probe, amplitudes, offsets, counts):
     half = probe.shape[-1] // 2
     core = lax.axis_index(TILE) % 2
     odd = lax.axis_index(POS) % 2
@@ -448,17 +449,25 @@
     def pick(where, when_zero, when_one):
         return jnp.where(where == 0, when_zero, when_one)
 
-    top, bottom = by_column(object_slices[:, :, :half]), by_column(object_slices[:, :, half:])
-    row_a = swap(pick(odd, bottom, top), POS, 0)
-    row_b = swap(pick(odd, top, bottom), POS, 1)
     west, east = object_slices[..., :half], object_slices[..., half:]
-    side_in = swap(pick(core, east, west), TILE, 0)
-    side_out = swap(pick(core, west, east), TILE, 1)
-    ends_out = swap(jnp.stack([pick(core, row_a[0], row_a[1]), pick(core, row_b[0], row_b[1])]), TILE, 1)
-    ends_in = swap(jnp.stack([pick(core, row_a[1], row_a[0]), pick(core, row_b[1], row_b[0])]), TILE, 0)
-    amps = ordered(amplitudes[0, 0])
+    outer, inner = pick(core, west, east), pick(core, east, west)
+
+    def rows(columns, other):
+        return pick(other, columns[:, :, half:], columns[:, :, :half])
+
+    out_a = swap(rows(outer, odd), POS, 0)
+    out_b = swap(rows(outer, 1 - odd), POS, 1)
+    side_out = swap(outer, TILE, 1)
+    in_a = swap(rows(inner, odd), POS, 0)
+    in_b = swap(rows(inner, 1 - odd), POS, 1)
+    side_in = swap(inner, TILE, 0)
+    end_out_a = swap(out_a, TILE, 1)
+    end_out_b = swap(out_b, TILE, 1)
+    end_in_a = swap(in_a, TILE, 0)
+    end_in_b = swap(in_b, TILE, 0)
     end_in, end_out, grad_in, grad_out, slabs, middle, probe_grad = gradients(
-        counts, offsets[0, 0], *by_core, object_slices, row_a, row_b, side_in, side_out, ends_in, ends_out, probe, amps, mats, mats_t
+        counts, offsets[0, 0].T, *by_core, object_slices, out_a, out_b, in_a, in_b, side_in, side_out,
+        end_in_a, end_in_b, end_out_a, end_out_b, probe, amplitudes[0, 0], mats, mats_t, perm,
     )
     end_out = swap(end_out, TILE, 1)
     end_in = swap(end_in, TILE, 0)
@@ -468,7 +477,7 @@
     row_a, row_b = merged_edges(*by_core, slabs, end_in, end_out)
     row_a = swap(row_a, POS, 0)
     row_b = swap(row_b, POS, 1)
-    object_grad = merged_core(*by_core, middle, grad_in, grad_out, row_a, row_b)
+    object_grad, probe_total = merged_core(*by_core, middle, grad_in, grad_out, row_a, row_b, probe_total)
     return (object_grad, probe_total)
 
 
@@ -485,7 +494,7 @@
     mats = jnp.asarray(halves(real))
     mats_t = jnp.asarray(halves(np.swapaxes(real, 1, 2)))
     return jax.shard_map(
-        functools.partial(shards, mats, mats_t),
+        functools.partial(shards, mats, mats_t, jnp.asarray(even_then_odd(256))),
         mesh=torus,
         in_specs=placed,
         out_specs=(P(None, None, POS, TILE), P()),

time: 115 us -> 114 us (level)
  blocking collectives: 19.1 us -> 0 us
  starting transfers between devices: 51.8 us -> 66.7 us
  waiting for transfers between devices: 11 us -> 23.8 us
  Pallas kernels: 22.3 us -> 15.9 us
  local copies, waits for them, and re-layouts: 5.12 us -> 3.05 us
    all_to_all x1 -> x0, blocking collectives: 19.1 us -> none  [total_over_devices(): lax.all_to_all(jnp.broadcast_to(mine, parts.shape), ALL, 0, 0, tiled=True)]
    all_to_all x0 -> x1, waiting for transfers between devices: none -> 13.6 us  [total_over_devices(): lax.all_to_all(jnp.broadcast_to(mine, parts.shape), ALL, 0, 0, tiled=True)]
    ppermute x12 -> x16, starting transfers between devices: 28.6 us -> 38.6 us  [swap(): lax.ppermute(value, axis, pairs + [(after, before) for before, after in p...]
    pallas_call x2 -> x1, Pallas kernels: 19.9 us -> 12.4 us  [gradients(): pl.pallas_call(main_kernel, in_specs=[smem] * 4 + [any_space] * 16, out_s...]
    all_to_all x0 -> x1, starting transfers between devices: none -> 5.66 us  [total_over_devices(): lax.all_to_all(jnp.broadcast_to(mine, parts.shape), ALL, 0, 0, tiled=True)]
    another operation x1 -> x0, local copies, waits for them, and re-layouts: 1.39 us -> none  [by_column(): return jnp.stack([rows[..., :half], rows[..., half:]])]
    unnamed x13 -> x24, local copies, waits for them, and re-layouts: 3.01 us -> 2.21 us
    ppermute x12 -> x16, waiting for transfers between devices: 5.96 us -> 5.92 us  [swap(): lax.ppermute(value, axis, pairs + [(after, before) for before, after in p...]
  transfers between devices with their start and end apart: 13 -> 18, of which waited for: 2 -> 5; matrix products, arithmetic and copies ran while one was open for 4% -> 2% of each run, Pallas kernels for 7% -> 1%
where the time goes in v1:
time: 114 us
  starting transfers between devices  66.7 us (59%)
  waiting for transfers between devices  23.8 us (21%)
  Pallas kernels  15.9 us (14%)
  local copies, waits for them, and re-layouts  3.05 us (3%)
  other arithmetic  2.54 us (2%)
  between operations  1.61 us (1%)
    ppermute x16, starting transfers between devices, swap(): lax.ppermute(value, axis, pairs + [(after, before) for before, after in p...  38.6 us
    all_to_all x1, starting transfers between devices, total_over_devices(): parts = lax.all_to_all(blocks, ALL, 0, 0, tiled=True)  22.4 us
    all_to_all x1, waiting for transfers between devices, total_over_devices(): lax.all_to_all(jnp.broadcast_to(mine, parts.shape), ALL, 0, 0, tiled=True)  13.6 us
    pallas_call x1, Pallas kernels, gradients(): pl.pallas_call(main_kernel, in_specs=[smem] * 4 + [any_space] * 16, out_s...  12.4 us
    ppermute x16, waiting for transfers between devices, swap(): lax.ppermute(value, axis, pairs + [(after, before) for before, after in p...  5.92 us
    all_to_all x1, starting transfers between devices, total_over_devices(): lax.all_to_all(jnp.broadcast_to(mine, parts.shape), ALL, 0, 0, tiled=True)  5.66 us
    all_to_all x1, waiting for transfers between devices, total_over_devices(): parts = lax.all_to_all(blocks, ALL, 0, 0, tiled=True)  4.3 us
  transfers between devices with their start and end apart: 18, of which 5 were waited for; matrix products, arithmetic and copies ran while one was open for 2% of the time, Pallas kernels for 1%

profile of v1, /device:TPU:1, one launch (start us, length us, event | category | flops | bytes accessed | tf_op | source)
XLA Modules:
  0.0 113.6 jit_solution(3986949024965121090)
XLA Ops:
  0.7 1.3 %slice_select_fusion = (f32[2,2,256,128]{3,2,1,0:T(8,128)S(1)}, f32[2,2,256,128]{3,2,1,0:T(8,128)S(1)}) fusion(f32[2,2,256,256]{3,2,1,0:T(8,128)} %own_ref.1, pred[]{:T(512)S(6)} %eq.16), kind=kLoop, calls=%fused_computation | loop fusion | flops 262144 | bytes 2097153 | tf_op jit(solution)/shard_map/jit(_where)/select_n | solution.py:450
  2.0 0.7 collective-permute-start.3
  2.7 5.4 %collective-permute-start.2 = (f32[2,2,128,128]{3,2,1,0:T(8,128)S(1)}, f32[2,2,128,128]{3,2,1,0:T(8,128)S(1)}, u32[]{:S(2)}, u32[]{:S(2)}) collective-permute-start(f32[2,2,128,128]{3,2,1,0:T(8,128)S(1)} %get-tuple-element.23), channel_id=1, source_target_pairs={{0,8},{16,24},{32,40},{48,56},{64,72},{80,88},{96,104},{112,120},{... | collective-permute-start | bytes 786440 | tf_op jit(solution)/shard_map/ppermute | solution.py:431
  8.1 0.7 collective-permute-start.1
  8.8 2.7 %collective-permute-start = (f32[2,2,128,128]{3,2,1,0:T(8,128)S(1)}, f32[2,2,128,128]{3,2,1,0:T(8,128)S(1)}, u32[]{:S(2)}, u32[]{:S(2)}) collective-permute-start(f32[2,2,128,128]{3,2,1,0:T(8,128)S(1)} %get-tuple-element.25), channel_id=1, source_target_pairs={{0,8},{16,24},{32,40},{48,56},{64,72},{80,88},{96,104},{112,120},{... | collective-permute-start | bytes 786440 | tf_op jit(solution)/shard_map/ppermute | solution.py:431
  11.5 1.7 %collective-permute-start.7 = (f32[2,2,128,128]{3,2,1,0:T(8,128)S(1)}, f32[2,2,128,128]{3,2,1,0:T(8,128)S(1)}, u32[]{:S(2)}, u32[]{:S(2)}) collective-permute-start(f32[2,2,128,128]{3,2,1,0:T(8,128)S(1)} %collective-permute-done.3.in_b_ref), channel_id=1, source_target_pairs={{0,1},{2,3},{4,5},{6,7},{1,0},{3,2},{5,4},{7,6},{8,9},{10,11},{12,... | collective-permute-start | bytes 786440 | tf_op jit(solution)/shard_map/ppermute | solution.py:431
  13.3 0.5 collective-permute-done.2.in_a_ref
  13.8 5.7 %collective-permute-start.5 = (f32[2,2,256,128]{3,2,1,0:T(8,128)S(1)}, f32[2,2,256,128]{3,2,1,0:T(8,128)S(1)}, u32[]{:S(2)}, u32[]{:S(2)}) collective-permute-start(f32[2,2,256,128]{3,2,1,0:T(8,128)S(1)} %get-tuple-element.21), channel_id=1, source_target_pairs={{1,2},{3,4},{5,6},{2,1},{4,3},{6,5},{9,10},{11,12},{13,14},{10,9},... | collective-permute-start | bytes 1572872 | tf_op jit(solution)/shard_map/ppermute | solution.py:431
  19.5 0.1 collective-permute-start.6
  19.6 4.3 %collective-permute-start.9 = (f32[2,2,128,128]{3,2,1,0:T(8,128)S(1)}, f32[2,2,128,128]{3,2,1,0:T(8,128)S(1)}, u32[]{:S(2)}, u32[]{:S(2)}) collective-permute-start(f32[2,2,128,128]{3,2,1,0:T(8,128)S(1)} %collective-permute-done.1.out_b_ref), channel_id=1, source_target_pairs={{1,2},{3,4},{5,6},{2,1},{4,3},{6,5},{9,10},{11,12},{13,14},{10,9},... | collective-permute-start | bytes 786440 | tf_op jit(solution)/shard_map/ppermute | solution.py:431
  24.0 1.9 %collective-permute-start.8 = (f32[2,2,128,128]{3,2,1,0:T(8,128)S(1)}, f32[2,2,128,128]{3,2,1,0:T(8,128)S(1)}, u32[]{:S(2)}, u32[]{:S(2)}) collective-permute-start(f32[2,2,128,128]{3,2,1,0:T(8,128)S(1)} %collective-permute-done.out_a_ref), channel_id=1, source_target_pairs={{1,2},{3,4},{5,6},{2,1},{4,3},{6,5},{9,10},{11,12},{13,14},{10,9},... | collective-permute-start | bytes 786440 | tf_op jit(solution)/shard_map/ppermute | solution.py:431
  26.6 2.6 %collective-permute-done.9.end_out_b_ref = f32[2,2,128,128]{3,2,1,0:T(8,128)S(1)} collective-permute-done((f32[2,2,128,128]{3,2,1,0:T(8,128)S(1)}, f32[2,2,128,128]{3,2,1,0:T(8,128)S(1)}, u32[]{:S(2)}, u32[]{:S(2)}) %collective-permute-start.9) | collective-permute-done | bytes 262176 | tf_op jit(solution)/shard_map/ppermute | solution.py:431
  29.1 2.8 %collective-permute-done.8.end_out_a_ref = f32[2,2,128,128]{3,2,1,0:T(8,128)S(1)} collective-permute-done((f32[2,2,128,128]{3,2,1,0:T(8,128)S(1)}, f32[2,2,128,128]{3,2,1,0:T(8,128)S(1)}, u32[]{:S(2)}, u32[]{:S(2)}) %collective-permute-start.8) | collective-permute-done | bytes 262176 | tf_op jit(solution)/shard_map/ppermute | solution.py:431
  32.0 0.6 copy-done.11
  32.7 0.2 copy-done.2
  32.8 0.2 copy-done.3
  33.0 12.4 %slot_gradients.1 = (f32[2,2,2,128,128]{4,3,2,1,0:T(8,128)}, f32[2,2,2,128,128]{4,3,2,1,0:T(8,128)}, f32[2,2,256,128]{3,2,1,0:T(8,128)}, f32[2,2,256,128]{3,2,1,...) custom-call(s32[1,1]{1,0:T(1,128)S(6)} %copy.10.count_ref, ...), custom_call_target="tpu_custom_call" | custom-call | flops 12884901888 | bytes 16777216 | tf_op jit(solution)/shard_map/slot_gradients/pallas_call | solution.py:345
  45.4 0.1 collective-permute-start.12
  45.5 8.8 %collective-permute-start.13 = (f32[2,2,2,128,128]{4,3,2,1,0:T(8,128)}, f32[2,2,2,128,128]{4,3,2,1,0:T(8,128)S(1)}, u32[]{:S(2)}, u32[]{:S(2)}) collective-permute-start(f32[2,2,2,128,128]{4,3,2,1,0:T(8,128)} %get-tuple-element.16), channel_id=1, source_target_pairs={{1,2},{3,4},{5,6},{2,1},{4,3},{6,5},{9,10},{11,12},{13,14},{10,9},... | collective-permute-start | bytes 1572872 | tf_op jit(solution)/shard_map/ppermute | solution.py:431
  54.3 22.4 %all-to-all-start = ((f32[128,8,128]{2,1,0:T(8,128)}), f32[128,8,128]{2,1,0:T(8,128)}, u32[]{:S(2)}, u32[]{:S(2)}) async-start(f32[128,8,128]{2,1,0:T(8,128)} %bitcast.17), calls=%async_computation | async-start | bytes 1048576 | tf_op jit(solution)/shard_map/all_to_all | solution.py:437
  76.8 1.2 %collective-permute-start.10 = (f32[2,2,256,128]{3,2,1,0:T(8,128)}, f32[2,2,256,128]{3,2,1,0:T(8,128)S(1)}, u32[]{:S(2)}, u32[]{:S(2)}) collective-permute-start(f32[2,2,256,128]{3,2,1,0:T(8,128)} %get-tuple-element.12), channel_id=1, source_target_pairs={{0,1},{2,3},{4,5},{6,7},{1,0},{3,2},{5,4},{7,6},{8,9},{10,11},{12,... | collective-permute-start | bytes 1572872 | tf_op jit(solution)/shard_map/ppermute | solution.py:431
  78.0 2.5 %collective-permute-start.11 = (f32[2,2,256,128]{3,2,1,0:T(8,128)}, f32[2,2,256,128]{3,2,1,0:T(8,128)S(1)}, u32[]{:S(2)}, u32[]{:S(2)}) collective-permute-start(f32[2,2,256,128]{3,2,1,0:T(8,128)} %get-tuple-element.13), channel_id=1, source_target_pairs={{1,2},{3,4},{5,6},{2,1},{4,3},{6,5},{9,10},{11,12},{13,14},{10,9},... | collective-permute-start | bytes 1572872 | tf_op jit(solution)/shard_map/ppermute | solution.py:431
  80.5 1.2 %copy-done = f32[2,2,2,2,128,128]{5,4,3,2,1,0:T(8,128)S(1)} copy-done((f32[2,2,2,2,128,128]{5,4,3,2,1,0:T(8,128)S(1)}, f32[2,2,2,2,128,128]{5,4,3,2,1,0:T(8,128)}, u32[]{:S(2)}) %copy-start) | copy-done | bytes 1048600
  81.7 1.2 %merge_edges.1 = (f32[2,2,2,128,128]{4,3,2,1,0:T(8,128)}, f32[2,2,2,128,128]{4,3,2,1,0:T(8,128)}) custom-call(s32[1]{0:T(128)} %bitcast.core_at, s32[1]{0:T(128)} %bitcast.1.odd_at, f32[2,2,2,2,128,128]{5,4,3,2,1,0:T(8,128)S(1)} %copy-done, f32[2,2,2,128,128]{4,3,2,1,0:T(8,128)S(1)} %collective-permute-done.12.in_ref, ...), custom_call_target="tpu_custom_call" | custom-call | flops 262144 | bytes 3145728 | tf_op jit(solution)/shard_map/merge_edges/pallas_call | solution.py:387
  82.9 1.3 %collective-permute-start.14 = (f32[2,2,2,128,128]{4,3,2,1,0:T(8,128)}, f32[2,2,2,128,128]{4,3,2,1,0:T(8,128)S(1)}, u32[]{:S(2)}, u32[]{:S(2)}) collective-permute-start(f32[2,2,2,128,128]{4,3,2,1,0:T(8,128)} %get-tuple-element.17), channel_id=1, source_target_pairs={{0,8},{16,24},{32,40},{48,56},{64,72},{80,88},{96,104},{112,120},{... | collective-permute-start | bytes 1572872 | tf_op jit(solution)/shard_map/ppermute | solution.py:431
  84.3 1.4 %collective-permute-start.15 = (f32[2,2,2,128,128]{4,3,2,1,0:T(8,128)}, f32[2,2,2,128,128]{4,3,2,1,0:T(8,128)}, u32[]{:S(2)}, u32[]{:S(2)}) collective-permute-start(f32[2,2,2,128,128]{4,3,2,1,0:T(8,128)} %get-tuple-element.18), channel_id=1, source_target_pairs={{8,16},{24,32},{40,48},{56,64},{72,80},{88,96},{104,112},{16,8},{3... | collective-permute-start | bytes 1572872 | tf_op jit(solution)/shard_map/ppermute | solution.py:431
  85.7 4.3 %all-to-all-done = f32[128,8,128]{2,1,0:T(8,128)} async-done(((f32[128,8,128]{2,1,0:T(8,128)}), f32[128,8,128]{2,1,0:T(8,128)}, u32[]{:S(2)}, u32[]{:S(2)}) %all-to-all-start) | async-done | bytes 524320 | tf_op jit(solution)/shard_map/all_to_all | solution.py:437
  90.0 1.2 %reduce_sum.9 = f32[8,128]{1,0:T(8,128)S(1)} reduce(f32[128,8,128]{2,1,0:T(8,128)} %all-to-all-done, f32[]{:T(128)} %constant.43.clone.1), dimensions={0}, to_apply=%region_0.1 | reduce | flops 130048 | bytes 528388 | tf_op jit(solution)/shard_map/reduce_sum | solution.py:438
  91.2 0.8 broadcast_in_dim.2
  92.0 5.7 %all-to-all-start.1 = ((f32[128,8,128]{2,1,0:T(8,128)}), f32[128,8,128]{2,1,0:T(8,128)S(1)}, u32[]{:S(2)}, u32[]{:S(2)}) async-start(f32[128,8,128]{2,1,0:T(8,128)} %broadcast_in_dim.2), calls=%async_computation.1 | async-start | bytes 1048576 | tf_op jit(solution)/shard_map/all_to_all | solution.py:439
  97.7 13.6 %all-to-all-done.1 = f32[128,8,128]{2,1,0:T(8,128)S(1)} async-done(((f32[128,8,128]{2,1,0:T(8,128)}), f32[128,8,128]{2,1,0:T(8,128)S(1)}, u32[]{:S(2)}, u32[]{:S(2)}) %all-to-all-start.1) | async-done | bytes 524320 | tf_op jit(solution)/shard_map/all_to_all | solution.py:439
  111.3 2.3 %merge_core.1 = (f32[2,2,256,256]{3,2,1,0:T(8,128)}, f32[2,256,256]{2,1,0:T(8,128)}) custom-call(s32[1]{0:T(128)} %bitcast.core_at, s32[1]{0:T(128)} %bitcast.1.odd_at, f32[2,2,2,256,128]{4,3,2,1,0:T(8,128)S(1)} %copy-done.1, f32[2,2,256,128]{3,2,1,0:T(8,128)S(1)} %collective-permute-done.10.in_ref, f32[2,2,256,128]{3,2,1,0:T(8,128)S(1)} %collective-permute-done.11.out_ref, ...), custom_call_target="tpu_custom_call" | custom-call | flops 524288 | bytes 4194304 | tf_op jit(solution)/shard_map/merge_core/pallas_call | solution.py:417
  (36 shorter events, 0.2 us)
Async XLA Ops:
  2.0 9.5 %collective-permute-start.3 = (f32[2,2,128,128]{3,2,1,0:T(8,128)S(1)}, f32[2,2,128,128]{3,2,1,0:T(8,128)S(1)}, u32[]{:S(2)}, u32[]{:S(2)}) collective-permute-start(f32[2,2,128,128]{3,2,1,0:T(8,128)S(1)} %get-tuple-element.22), channel_id=1, source_target_pairs={{8,16},{24,32},{40,48},{56,64},{72,80},{88,96},{104,112},{16,8},{3... | collective-permute-start | bytes 786440 | tf_op jit(solution)/shard_map/ppermute | solution.py:431
  2.7 11.1 %collective-permute-start.2 = (f32[2,2,128,128]{3,2,1,0:T(8,128)S(1)}, f32[2,2,128,128]{3,2,1,0:T(8,128)S(1)}, u32[]{:S(2)}, u32[]{:S(2)}) collective-permute-start(f32[2,2,128,128]{3,2,1,0:T(8,128)S(1)} %get-tuple-element.23), channel_id=1, source_target_pairs={{0,8},{16,24},{32,40},{48,56},{64,72},{80,88},{96,104},{112,120},{... | collective-permute-start | bytes 786440 | tf_op jit(solution)/shard_map/ppermute | solution.py:431
  8.1 11.4 %collective-permute-start.1 = (f32[2,2,128,128]{3,2,1,0:T(8,128)S(1)}, f32[2,2,128,128]{3,2,1,0:T(8,128)S(1)}, u32[]{:S(2)}, u32[]{:S(2)}) collective-permute-start(f32[2,2,128,128]{3,2,1,0:T(8,128)S(1)} %get-tuple-element.24), channel_id=1, source_target_pairs={{8,16},{24,32},{40,48},{56,64},{72,80},{88,96},{104,112},{16,8},{3... | collective-permute-start | bytes 786440 | tf_op jit(solution)/shard_map/ppermute | solution.py:431
  8.8 10.8 %collective-permute-start = (f32[2,2,128,128]{3,2,1,0:T(8,128)S(1)}, f32[2,2,128,128]{3,2,1,0:T(8,128)S(1)}, u32[]{:S(2)}, u32[]{:S(2)}) collective-permute-start(f32[2,2,128,128]{3,2,1,0:T(8,128)S(1)} %get-tuple-element.25), channel_id=1, source_target_pairs={{0,8},{16,24},{32,40},{48,56},{64,72},{80,88},{96,104},{112,120},{... | collective-permute-start | bytes 786440 | tf_op jit(solution)/shard_map/ppermute | solution.py:431
  11.5 20.5 %copy-start.4 = (f32[2,2,128,128]{3,2,1,0:T(8,128)}, f32[2,2,128,128]{3,2,1,0:T(8,128)S(1)}, u32[]{:S(2)}) copy-start(f32[2,2,128,128]{3,2,1,0:T(8,128)S(1)} %collective-permute-done.3.in_b_ref) | copy-start | bytes 786436
  11.5 12.5 %collective-permute-start.7 = (f32[2,2,128,128]{3,2,1,0:T(8,128)S(1)}, f32[2,2,128,128]{3,2,1,0:T(8,128)S(1)}, u32[]{:S(2)}, u32[]{:S(2)}) collective-permute-start(f32[2,2,128,128]{3,2,1,0:T(8,128)S(1)} %collective-permute-done.3.in_b_ref), channel_id=1, source_target_pairs={{0,1},{2,3},{4,5},{6,7},{1,0},{3,2},{5,4},{7,6},{8,9},{10,11},{12,... | collective-permute-start | bytes 786440 | tf_op jit(solution)/shard_map/ppermute | solution.py:431
  13.2 18.8 %collective-permute-start.4 = (f32[2,2,256,128]{3,2,1,0:T(8,128)S(1)}, f32[2,2,256,128]{3,2,1,0:T(8,128)S(1)}, u32[]{:S(2)}, u32[]{:S(2)}) collective-permute-start(f32[2,2,256,128]{3,2,1,0:T(8,128)S(1)} %get-tuple-element.20), channel_id=1, source_target_pairs={{0,1},{2,3},{4,5},{6,7},{1,0},{3,2},{5,4},{7,6},{8,9},{10,11},{12,... | collective-permute-start | bytes 1572872 | tf_op jit(solution)/shard_map/ppermute | solution.py:431
  13.8 18.2 %copy-start.5 = (f32[2,2,128,128]{3,2,1,0:T(8,128)}, f32[2,2,128,128]{3,2,1,0:T(8,128)S(1)}, u32[]{:S(2)}) copy-start(f32[2,2,128,128]{3,2,1,0:T(8,128)S(1)} %collective-permute-done.2.in_a_ref) | copy-start | bytes 786436
  13.8 18.1 %collective-permute-start.5 = (f32[2,2,256,128]{3,2,1,0:T(8,128)S(1)}, f32[2,2,256,128]{3,2,1,0:T(8,128)S(1)}, u32[]{:S(2)}, u32[]{:S(2)}) collective-permute-start(f32[2,2,256,128]{3,2,1,0:T(8,128)S(1)} %get-tuple-element.21), channel_id=1, source_target_pairs={{1,2},{3,4},{5,6},{2,1},{4,3},{6,5},{9,10},{11,12},{13,14},{10,9},... | collective-permute-start | bytes 1572872 | tf_op jit(solution)/shard_map/ppermute | solution.py:431
  19.5 12.5 %copy-start.6 = (f32[2,2,128,128]{3,2,1,0:T(8,128)}, f32[2,2,128,128]{3,2,1,0:T(8,128)S(1)}, u32[]{:S(2)}) copy-start(f32[2,2,128,128]{3,2,1,0:T(8,128)S(1)} %collective-permute-done.1.out_b_ref) | copy-start | bytes 786436
  19.5 7.1 %collective-permute-start.6 = (f32[2,2,128,128]{3,2,1,0:T(8,128)S(1)}, f32[2,2,128,128]{3,2,1,0:T(8,128)S(1)}, u32[]{:S(2)}, u32[]{:S(2)}) collective-permute-start(f32[2,2,128,128]{3,2,1,0:T(8,128)S(1)} %collective-permute-done.2.in_a_ref), channel_id=1, source_target_pairs={{0,1},{2,3},{4,5},{6,7},{1,0},{3,2},{5,4},{7,6},{8,9},{10,11},{12,... | collective-permute-start | bytes 786440 | tf_op jit(solution)/shard_map/ppermute | solution.py:431
  19.6 12.4 %copy-start.7 = (f32[2,2,128,128]{3,2,1,0:T(8,128)}, f32[2,2,128,128]{3,2,1,0:T(8,128)S(1)}, u32[]{:S(2)}) copy-start(f32[2,2,128,128]{3,2,1,0:T(8,128)S(1)} %collective-permute-done.out_a_ref) | copy-start | bytes 786436
  19.6 9.5 %collective-permute-start.9 = (f32[2,2,128,128]{3,2,1,0:T(8,128)S(1)}, f32[2,2,128,128]{3,2,1,0:T(8,128)S(1)}, u32[]{:S(2)}, u32[]{:S(2)}) collective-permute-start(f32[2,2,128,128]{3,2,1,0:T(8,128)S(1)} %collective-permute-done.1.out_b_ref), channel_id=1, source_target_pairs={{1,2},{3,4},{5,6},{2,1},{4,3},{6,5},{9,10},{11,12},{13,14},{10,9},... | collective-permute-start | bytes 786440 | tf_op jit(solution)/shard_map/ppermute | solution.py:431
  24.0 8.0 %copy-start.8 = (f32[2,2,128,128]{3,2,1,0:T(8,128)}, f32[2,2,128,128]{3,2,1,0:T(8,128)S(1)}, u32[]{:S(2)}) copy-start(f32[2,2,128,128]{3,2,1,0:T(8,128)S(1)} %collective-permute-done.7.end_in_b_ref) | copy-start | bytes 786436
  24.0 8.0 %collective-permute-start.8 = (f32[2,2,128,128]{3,2,1,0:T(8,128)S(1)}, f32[2,2,128,128]{3,2,1,0:T(8,128)S(1)}, u32[]{:S(2)}, u32[]{:S(2)}) collective-permute-start(f32[2,2,128,128]{3,2,1,0:T(8,128)S(1)} %collective-permute-done.out_a_ref), channel_id=1, source_target_pairs={{1,2},{3,4},{5,6},{2,1},{4,3},{6,5},{9,10},{11,12},{13,14},{10,9},... | collective-permute-start | bytes 786440 | tf_op jit(solution)/shard_map/ppermute | solution.py:431
  26.6 5.5 %copy-start.9 = (f32[2,2,128,128]{3,2,1,0:T(8,128)}, f32[2,2,128,128]{3,2,1,0:T(8,128)S(1)}, u32[]{:S(2)}) copy-start(f32[2,2,128,128]{3,2,1,0:T(8,128)S(1)} %collective-permute-done.6.end_in_a_ref) | copy-start | bytes 786436
  29.1 2.9 %copy-start.10 = (f32[2,2,128,128]{3,2,1,0:T(8,128)}, f32[2,2,128,128]{3,2,1,0:T(8,128)S(1)}, u32[]{:S(2)}) copy-start(f32[2,2,128,128]{3,2,1,0:T(8,128)S(1)} %collective-permute-done.9.end_out_b_ref) | copy-start | bytes 786436
  31.9 0.7 copy-start.11
  32.0 0.9 copy-start.2
  32.0 1.0 copy-start.3
  45.4 35.1 %collective-permute-start.12 = (f32[2,2,2,128,128]{4,3,2,1,0:T(8,128)}, f32[2,2,2,128,128]{4,3,2,1,0:T(8,128)S(1)}, u32[]{:S(2)}, u32[]{:S(2)}) collective-permute-start(f32[2,2,2,128,128]{4,3,2,1,0:T(8,128)} %get-tuple-element.15), channel_id=1, source_target_pairs={{0,1},{2,3},{4,5},{6,7},{1,0},{3,2},{5,4},{7,6},{8,9},{10,11},{12,... | collective-permute-start | bytes 1572872 | tf_op jit(solution)/shard_map/ppermute | solution.py:431
  45.5 35.0 %collective-permute-start.13 = (f32[2,2,2,128,128]{4,3,2,1,0:T(8,128)}, f32[2,2,2,128,128]{4,3,2,1,0:T(8,128)S(1)}, u32[]{:S(2)}, u32[]{:S(2)}) collective-permute-start(f32[2,2,2,128,128]{4,3,2,1,0:T(8,128)} %get-tuple-element.16), channel_id=1, source_target_pairs={{1,2},{3,4},{5,6},{2,1},{4,3},{6,5},{9,10},{11,12},{13,14},{10,9},... | collective-permute-start | bytes 1572872 | tf_op jit(solution)/shard_map/ppermute | solution.py:431
  54.3 35.7 %all-to-all-start = ((f32[128,8,128]{2,1,0:T(8,128)}), f32[128,8,128]{2,1,0:T(8,128)}, u32[]{:S(2)}, u32[]{:S(2)}) async-start(f32[128,8,128]{2,1,0:T(8,128)} %bitcast.17), calls=%async_computation | async-start | bytes 1048576 | tf_op jit(solution)/shard_map/all_to_all | solution.py:437
  76.8 20.9 %collective-permute-start.10 = (f32[2,2,256,128]{3,2,1,0:T(8,128)}, f32[2,2,256,128]{3,2,1,0:T(8,128)S(1)}, u32[]{:S(2)}, u32[]{:S(2)}) collective-permute-start(f32[2,2,256,128]{3,2,1,0:T(8,128)} %get-tuple-element.12), channel_id=1, source_target_pairs={{0,1},{2,3},{4,5},{6,7},{1,0},{3,2},{5,4},{7,6},{8,9},{10,11},{12,... | collective-permute-start | bytes 1572872 | tf_op jit(solution)/shard_map/ppermute | solution.py:431
  78.0 19.7 %collective-permute-start.11 = (f32[2,2,256,128]{3,2,1,0:T(8,128)}, f32[2,2,256,128]{3,2,1,0:T(8,128)S(1)}, u32[]{:S(2)}, u32[]{:S(2)}) collective-permute-start(f32[2,2,256,128]{3,2,1,0:T(8,128)} %get-tuple-element.13), channel_id=1, source_target_pairs={{1,2},{3,4},{5,6},{2,1},{4,3},{6,5},{9,10},{11,12},{13,14},{10,9},... | collective-permute-start | bytes 1572872 | tf_op jit(solution)/shard_map/ppermute | solution.py:431
  80.5 1.2 %copy-start = (f32[2,2,2,2,128,128]{5,4,3,2,1,0:T(8,128)S(1)}, f32[2,2,2,2,128,128]{5,4,3,2,1,0:T(8,128)}, u32[]{:S(2)}) copy-start(f32[2,2,2,2,128,128]{5,4,3,2,1,0:T(8,128)} %get-tuple-element.14.slab_ref) | copy-start | bytes 3145732
  81.7 29.6 %copy-start.1 = (f32[2,2,2,256,128]{4,3,2,1,0:T(8,128)S(1)}, f32[2,2,2,256,128]{4,3,2,1,0:T(8,128)}, u32[]{:S(2)}) copy-start(f32[2,2,2,256,128]{4,3,2,1,0:T(8,128)} %get-tuple-element.11.core_ref) | copy-start | bytes 3145732
  82.9 28.4 %collective-permute-start.14 = (f32[2,2,2,128,128]{4,3,2,1,0:T(8,128)}, f32[2,2,2,128,128]{4,3,2,1,0:T(8,128)S(1)}, u32[]{:S(2)}, u32[]{:S(2)}) collective-permute-start(f32[2,2,2,128,128]{4,3,2,1,0:T(8,128)} %get-tuple-element.17), channel_id=1, source_target_pairs={{0,8},{16,24},{32,40},{48,56},{64,72},{80,88},{96,104},{112,120},{... | collective-permute-start | bytes 1572872 | tf_op jit(solution)/shard_map/ppermute | solution.py:431
  84.3 27.1 %collective-permute-start.15 = (f32[2,2,2,128,128]{4,3,2,1,0:T(8,128)}, f32[2,2,2,128,128]{4,3,2,1,0:T(8,128)}, u32[]{:S(2)}, u32[]{:S(2)}) collective-permute-start(f32[2,2,2,128,128]{4,3,2,1,0:T(8,128)} %get-tuple-element.18), channel_id=1, source_target_pairs={{8,16},{24,32},{40,48},{56,64},{72,80},{88,96},{104,112},{16,8},{3... | collective-permute-start | bytes 1572872 | tf_op jit(solution)/shard_map/ppermute | solution.py:431
  92.0 19.3 %all-to-all-start.1 = ((f32[128,8,128]{2,1,0:T(8,128)}), f32[128,8,128]{2,1,0:T(8,128)S(1)}, u32[]{:S(2)}, u32[]{:S(2)}) async-start(f32[128,8,128]{2,1,0:T(8,128)} %broadcast_in_dim.2), calls=%async_computation.1 | async-start | bytes 1048576 | tf_op jit(solution)/shard_map/all_to_all | solution.py:439
